TPU v7x, 256 devices: a whole 4x4x8 slice. The times are simulated.
256 devices in a mesh: outer: 16 (over z, core), inner: 16 (over y, x).
Axes of the slice: x: 4, y: 4, z: 8, core: 2. Of those that a mesh axis runs over, the one named last changes fastest.
Arguments:
- queries: bfloat16 [32768, 4096], P(('outer', 'inner')), may hold values from -48 to 48
- keys: bfloat16 [32768, 1024], P(('outer', 'inner')), may hold values from -20 to 20
- values: bfloat16 [32768, 1024], P(('outer', 'inner')), may hold values from -6 to 6
- ancestors: int32 [256, 8], replicated, may hold values from -1 to 255, as said below
- token_block: int32 [32768], replicated, may hold values from 0 to 255, as said below
- positions: int32 [32768], replicated, may hold values from 0 to 1023, as said below
Outputs:
- attended: bfloat16 [32768, 4096], P(('outer', 'inner'))
Inputs may be any that keep to these rules, and one draw needn't show every extreme that they name: `ancestors`: row b lists the blocks on the path from the root block 0 to block b, root first and b last, then -1; a parent has a smaller number than its child; some row lists 8 blocks. `token_block`: each aligned span of 128 tokens belongs to one block, and every block fills exactly one span; apart from block 0, no two blocks of one root path lie in the same aligned group of 2048 tokens. `positions`: a token's position is 128 times (the number of blocks on its block's root path minus 1) plus its offset within its span.
All inputs are finite; a program needn't handle non-finite values.
Results may differ from a plain program's by a relative error of at most 0.0065.
Values may be sent and summed in bfloat16 or wider, within the bound.
No kernel may reach another device: no remote copies, remote signals or barrier semaphores. Data moves between devices by JAX's collectives and lax.ppermute only.
A program may use at most 128 MiB of HBM per device.

v0:
```python
import functools

import jax
import jax.numpy as jnp
import numpy as np
from jax import lax
from jax.experimental import pallas as pl
from jax.experimental.pallas import tpu as pltpu
from jax.sharding import Mesh
from jax.sharding import PartitionSpec as P


HEADS = 32
KV_HEADS = 8
GROUP = HEADS // KV_HEADS
HEAD_DIM = 128
BLOCK = 128
ANC_MAX = 8
SLOTS = ANC_MAX - 1
DEVICES = 256
PLANES = 8
CAP = 34
HALF = BLOCK // 2
SHIFTS = ((0, 1, 7, 2), (6, 3, 5, 4))
GROUPS = len(SHIFTS)
KV_SCRATCH = [
    pltpu.VMEM((ANC_MAX * BLOCK, HEAD_DIM), jnp.bfloat16),
    pltpu.VMEM((ANC_MAX * BLOCK, 2 * HEAD_DIM), jnp.bfloat16),
]
PACK = (GROUP + 2) * HEAD_DIM
ROTARY_BASE = 500000.0
AXES = ("z", "c", "y", "xh", "xl")
HEAD_AXES = ("y", "xl")
NEG = -1e30
EXP2_SCALE = float(HEAD_DIM**-0.5 * np.log2(np.e))

HBM = pl.BlockSpec(memory_space=pltpu.HBM)
SMEM = pl.BlockSpec(memory_space=pltpu.SMEM)
VMEM = pl.BlockSpec(memory_space=pltpu.VMEM)
VMEM_ONE = pl.BlockSpec((1, 1), lambda h: (0, 0))


def room(mib):
    return pltpu.CompilerParams(vmem_limit_bytes=mib << 20)


def inverse_row():
    half = HEAD_DIM // 2
    inv = (ROTARY_BASE ** (-2.0 * np.arange(half, dtype=np.float64) / HEAD_DIM)).astype(np.float32)
    return np.concatenate([inv, inv])[None, :]


def turn(x, cosine, sine):
    x = x.astype(jnp.float32)
    return (x * cosine + pltpu.roll(x, HEAD_DIM // 2, 1) * sine).astype(jnp.bfloat16)


def device_index():
    z, c, y, xh, xl = [lax.axis_index(name) for name in AXES]
    return (((z * 2 + c) * 4 + y) * 2 + xh) * 2 + xl


def spread_kernel(
    pos_ref, inv_ref, k_hbm, v_hbm, send_ref, cos_ref, sin_ref, own_ref, v_ref, base_ref, sems
):
    start = pl.multiple_of(device_index() * BLOCK, BLOCK)
    loads = [
        pltpu.make_async_copy(pos_ref.at[pl.ds(start, BLOCK)], base_ref, sems.at[0]),
        pltpu.make_async_copy(k_hbm, own_ref, sems.at[1]),
        pltpu.make_async_copy(v_hbm, v_ref, sems.at[2]),
    ]
    for load in loads:
        load.start()
    loads[0].wait()
    rows = lax.broadcasted_iota(jnp.int32, (BLOCK, HEAD_DIM), 0) + base_ref[0]
    lanes = lax.broadcasted_iota(jnp.int32, (BLOCK, HEAD_DIM), 1)
    angles = rows.astype(jnp.float32) * inv_ref[...]
    cosine = jnp.cos(angles)
    sine = jnp.sin(angles)
    sine = jnp.where(lanes < HEAD_DIM // 2, -sine, sine)
    cos_ref[...] = cosine
    sin_ref[...] = sine
    loads[1].wait()
    loads[2].wait()
    for h in range(KV_HEADS):
        cols = slice(h * HEAD_DIM, (h + 1) * HEAD_DIM)
        turned = turn(own_ref[:, cols], cosine, sine)
        own_ref[:, cols] = turned
        plain = v_ref[:, cols]
        for high in range(2):
            for low in range(8):
                t = (high * 8 + low) * 8
                send_ref[low, 0, h // 2, high, h % 2] = turned[t : t + 8]
                send_ref[low, 1, h // 2, high, h % 2] = plain[t : t + 8]


def bundle_kernel(count_ref, cos_ref, sin_ref, q_ref, k_ref, v_ref, out_ref):
    for g in range(GROUP):
        cols = slice(g * HEAD_DIM, (g + 1) * HEAD_DIM)
        out_ref[:, cols] = turn(q_ref[:, cols], cos_ref[...], sin_ref[...])
    out_ref[:, GROUP * HEAD_DIM : (GROUP + 1) * HEAD_DIM] = k_ref[...]
    out_ref[:, (GROUP + 1) * HEAD_DIM :] = v_ref[...]


def plan_kernel(token_ref, anc_ref, picks_ref, slots_ref, count_ref):
    n = DEVICES
    f32, bf, i32 = jnp.float32, jnp.bfloat16, jnp.int32
    across = (((1,), (1,)), ((), ()))
    anc = anc_ref[...]
    col = token_ref[:, 0:1]
    lane = lax.broadcasted_iota(i32, (n, n), 1)
    sub = lax.broadcasted_iota(i32, (n, n), 0)
    row = jnp.sum(jnp.where(sub == lane, col, 0), axis=0, keepdims=True)
    depth = jnp.sum((anc >= 0).astype(i32), axis=0, keepdims=True)
    holds = jnp.zeros((n, n), f32)
    for j in range(SLOTS):
        entry = jnp.where(j < depth - 1, anc[j : j + 1], -1)
        holds = jnp.where(entry == col, 1.0, holds)
    block_at = (col == lane).astype(f32).astype(bf)
    plane8 = lax.broadcasted_iota(i32, (PLANES, n), 0)
    lane8 = lax.broadcasted_iota(i32, (PLANES, n), 1)
    in_plane = (lane8 // (n // PLANES) == plane8).astype(f32).astype(bf)
    blocks = jnp.dot(in_plane, block_at, preferred_element_type=f32)
    need = lax.dot_general(
        blocks.astype(bf), holds.astype(bf), across, preferred_element_type=f32
    )
    needed = (need > 0.5).astype(f32)
    upto = (sub <= lane).astype(f32).astype(bf)
    ranks = jnp.dot(needed.astype(bf), upto, preferred_element_type=f32)
    count_ref[...] = jnp.max(ranks, axis=(0, 1), keepdims=True).astype(i32)
    ranks = ranks - 1.0
    wanted = lax.broadcasted_iota(i32, (CAP, n), 0).astype(f32)
    span = lax.broadcasted_iota(i32, (CAP, n), 1).astype(f32)
    for z in range(PLANES):
        hit = (ranks[z : z + 1] == wanted) & (needed[z : z + 1] > 0.5)
        picks_ref[:, z : z + 1] = jnp.sum(
            jnp.where(hit, span, 0.0), axis=1, keepdims=True
        ).astype(i32)
    z, c, xh = lax.axis_index("z"), lax.axis_index("c"), lax.axis_index("xh")
    mine = z * 32 + c * 16 + (plane8 // 2) * 4 + xh * 2 + plane8 % 2
    own_block = jnp.dot(
        (lane8 == mine).astype(f32).astype(bf), block_at, preferred_element_type=f32
    )
    path = lax.dot_general(
        own_block.astype(bf), anc.astype(f32).astype(bf), across, preferred_element_type=f32
    ).astype(i32)
    my_rank = jnp.sum(jnp.where(plane8 == z, ranks, 0.0), axis=0, keepdims=True)
    for j in range(SLOTS):
        slot = jnp.sum(
            jnp.where(path[:, j : j + 1] == row, my_rank, 0.0), axis=1, keepdims=True
        ).astype(i32)
        slots_ref[:, j : j + 1] = jnp.clip(slot, 0, CAP - 1)
    slots_ref[:, SLOTS:] = jnp.sum((path >= 0).astype(i32), axis=1, keepdims=True) - 1


def pack_kernel(picks_ref, src_ref, *out_refs):
    z = lax.axis_index("z")
    for d in range(PLANES):
        plane = lax.rem(z + d, PLANES)

        def one(k, carry):
            out_refs[d][k] = src_ref[picks_ref[k, plane]]
            return carry

        lax.fori_loop(0, CAP, one, 0, unroll=True)


def pick_kernel(idx_ref, src_ref, out_ref):
    def one(d, carry):
        for j in range(SLOTS):
            out_ref[d, j] = src_ref[idx_ref[d, j]]
        return carry

    lax.fori_loop(0, out_ref.shape[0], one, 0)


def attention(x_ref, k_ref, v_ref, alive, period, out_ref):
    k_ref[0:BLOCK] = x_ref[:, GROUP * HEAD_DIM : (GROUP + 1) * HEAD_DIM]
    v_ref[0:BLOCK, 0:HEAD_DIM] = x_ref[:, (GROUP + 1) * HEAD_DIM :]
    column = lax.broadcasted_iota(jnp.int32, (1, SLOTS * BLOCK), 1)
    bias = jnp.where((column // period) % SLOTS < alive, 0.0, NEG)
    row = lax.broadcasted_iota(jnp.int32, (BLOCK, BLOCK), 0)
    col = lax.broadcasted_iota(jnp.int32, (BLOCK, BLOCK), 1)
    causal = col <= row
    cols = [slice(g * HEAD_DIM, (g + 1) * HEAD_DIM) for g in range(GROUP)]
    scores = [
        lax.dot_general(
            x_ref[:, at], k_ref[...], (((1,), (1,)), ((), ())), preferred_element_type=jnp.float32
        )
        for at in cols
    ]
    scores = [
        jnp.concatenate([jnp.where(causal, s[:, :BLOCK], NEG), s[:, BLOCK:] + bias], axis=1)
        for s in scores
    ]
    tops = [jnp.max(s, axis=1, keepdims=True) for s in scores]
    weights = [
        jnp.exp2((s - top) * EXP2_SCALE).astype(jnp.bfloat16) for s, top in zip(scores, tops)
    ]
    for at, w in zip(cols, weights):
        mixed = jnp.dot(w, v_ref[...], preferred_element_type=jnp.float32)
        out_ref[:, at] = (mixed[:, :HEAD_DIM] / mixed[:, HEAD_DIM:]).astype(jnp.bfloat16)


def own_member():
    return lax.axis_index("y") * 2 + lax.axis_index("xl")


def fill(k_ref, v_ref, slots_ref, m, here, there):
    def copy(dst_ref, parts):
        for j in range(SLOTS):
            slot = slots_ref[m, j]
            at = (j + 1) * BLOCK
            for part in parts:
                size = part.shape[1]
                dst_ref[at : at + size, 0:HEAD_DIM] = part[slot]
                at += size

    core = lax.axis_index("c")

    @pl.when(core == 0)
    def _():
        copy(k_ref, here)
        copy(v_ref, there)

    @pl.when(core != 0)
    def _():
        copy(k_ref, there)
        copy(v_ref, here)


def span_kernel(mask, slots_ref, x_ref, *refs):
    here, there = refs[: 2 * GROUPS], refs[2 * GROUPS : 4 * GROUPS]
    out_refs, (k_ref, v_ref, done_ref) = refs[4 * GROUPS : -3], refs[-3:]
    v_ref[:, HEAD_DIM:] = jnp.ones((ANC_MAX * BLOCK, HEAD_DIM), jnp.bfloat16)

    def one(n, carry):
        m = own_member() ^ mask ^ n
        fill(k_ref, v_ref, slots_ref, m, here, there)
        attention(x_ref.at[m], k_ref, v_ref, slots_ref[m, SLOTS], BLOCK, done_ref.at[n])
        return carry

    lax.fori_loop(0, len(out_refs), one, 0)
    for n, out_ref in enumerate(out_refs):
        out_ref[...] = done_ref[n]


def head_kernel(alive_ref, x_ref, far_k_ref, far_v_ref, out_ref, k_ref, v_ref):
    v_ref[:, HEAD_DIM:] = jnp.ones((ANC_MAX * BLOCK, HEAD_DIM), jnp.bfloat16)
    k_ref[BLOCK:] = far_k_ref[...]
    v_ref[BLOCK:, 0:HEAD_DIM] = far_v_ref[...]
    attention(x_ref, k_ref, v_ref, alive_ref[0], HALF, out_ref)


def join_kernel(*refs):
    out_ref, sems = refs[-2], refs[-1]
    width = GROUP * HEAD_DIM
    copies = []
    for step in range(KV_HEADS):
        at = pl.multiple_of((own_member() ^ step) * width, width)
        copies.append(
            pltpu.make_async_copy(refs[step], out_ref.at[:, pl.ds(at, width)], sems.at[step])
        )
    for copy in copies:
        copy.start()
    for copy in copies:
        copy.wait()


def quick(picks, slots, chunks, members):
    bf = jnp.bfloat16
    packs = pl.pallas_call(
        pack_kernel,
        out_shape=[jax.ShapeDtypeStruct((CAP, 8, HEAD_DIM), bf)] * PLANES,
        in_specs=[SMEM, VMEM],
        compiler_params=room(8),
    )(picks, chunks)
    swap = [(0, 1), (1, 0)]
    got = {0: packs[0]}
    for shifts in SHIFTS:
        for d in shifts:
            if d:
                pairs = [(i, (i + d) % PLANES) for i in range(PLANES)]
                got[d] = lax.ppermute(packs[d], "z", pairs)
    near = [
        jnp.stack([got[d] for d in shifts], axis=1).reshape(CAP, 8 * len(shifts), HEAD_DIM)
        for shifts in SHIFTS
    ]
    far, near_there = [], []
    for part in near:
        far.append(lax.ppermute(part, "xh", swap))
        near_there.append(lax.ppermute(part, "c", swap))
    here = near + far
    there = near_there + [lax.ppermute(part, "c", swap) for part in far]
    outs = {}
    shape = (BLOCK, GROUP * HEAD_DIM)
    for mask in (4, 0):
        results = pl.pallas_call(
            functools.partial(span_kernel, mask),
            out_shape=[jax.ShapeDtypeStruct(shape, bf)] * 4,
            in_specs=[SMEM] + [VMEM] * (1 + 4 * GROUPS),
            out_specs=[VMEM] * 4,
            scratch_shapes=KV_SCRATCH + [pltpu.VMEM((4,) + shape, bf)],
            compiler_params=room(24),
            cost_estimate=pl.CostEstimate(
                flops=1 << 30, bytes_accessed=1 << 21, transcendentals=1 << 20
            ),
        )(slots, members, *here, *there)
        for n, out in enumerate(results):
            step = mask ^ n
            pairs = [(m, m ^ step) for m in range(KV_HEADS)]
            outs[step] = lax.ppermute(out, HEAD_AXES, pairs) if step else out
    return [outs[step] for step in range(KV_HEADS)]


def join(outs, *unused):
    return pl.pallas_call(
        join_kernel,
        out_shape=jax.ShapeDtypeStruct((BLOCK, HEADS * HEAD_DIM), jnp.bfloat16),
        in_specs=[VMEM] * KV_HEADS,
        out_specs=HBM,
        scratch_shapes=[pltpu.SemaphoreType.DMA((KV_HEADS,))],
        compiler_params=pltpu.CompilerParams(vmem_limit_bytes=67043328),
    )(*outs)


def general(outs, chunks, bundle, token_block, ancestors):
    bf = jnp.bfloat16
    span_blocks = token_block.reshape(DEVICES, BLOCK)[:, 0]
    ids = jnp.arange(DEVICES, dtype=jnp.int32)
    span_of = jnp.sum(jnp.where(span_blocks[:, None] == ids[None, :], ids[:, None], 0), axis=0)
    lineage = ancestors[span_blocks]
    depth = jnp.sum((lineage >= 0).astype(jnp.int32), axis=1)
    spans = span_of[jnp.maximum(lineage, 0)]
    alive = lax.dynamic_slice_in_dim(depth - 1, lax.axis_index(AXES), 1)
    packed = pl.pallas_call(
        pick_kernel,
        out_shape=jax.ShapeDtypeStruct((DEVICES, SLOTS, 8, HEAD_DIM), bf),
        in_specs=[SMEM, VMEM],
    )(spans, chunks)
    got = lax.all_to_all(packed.reshape(DEVICES, SLOTS * 8, HEAD_DIM), AXES, 0, 0, tiled=True)
    got = got.reshape(8, 2, 4, 2, 2, SLOTS, 8, HEAD_DIM).transpose(1, 2, 4, 3, 5, 0, 6, 7)
    got = got.reshape(2, KV_HEADS, SLOTS * BLOCK, HEAD_DIM)
    far_k = pl.BlockSpec((None, None, SLOTS * BLOCK, HEAD_DIM), lambda h: (0, h, 0, 0))
    far_v = pl.BlockSpec((None, None, SLOTS * BLOCK, HEAD_DIM), lambda h: (1, h, 0, 0))
    return pl.pallas_call(
        head_kernel,
        grid=(KV_HEADS,),
        out_shape=jax.ShapeDtypeStruct((BLOCK, HEADS * HEAD_DIM), bf),
        in_specs=[SMEM, pl.BlockSpec((None, BLOCK, PACK), lambda h: (h, 0, 0)), far_k, far_v],
        out_specs=pl.BlockSpec((BLOCK, GROUP * HEAD_DIM), lambda h: (0, h)),
        scratch_shapes=KV_SCRATCH,
    )(alive, bundle, got, got)


def shards(queries, keys, values, ancestors, token_block, positions):
    bf, f32, i32 = jnp.bfloat16, jnp.float32, jnp.int32
    send, cosine, sine, own_k = pl.pallas_call(
        spread_kernel,
        out_shape=(
            jax.ShapeDtypeStruct((8, 2, 4, 2, 2, 8, HEAD_DIM), bf),
            jax.ShapeDtypeStruct((BLOCK, HEAD_DIM), f32),
            jax.ShapeDtypeStruct((BLOCK, HEAD_DIM), f32),
            jax.ShapeDtypeStruct((BLOCK, KV_HEADS * HEAD_DIM), bf),
        ),
        in_specs=[HBM, VMEM, HBM, HBM],
        scratch_shapes=[
            pltpu.VMEM((BLOCK, KV_HEADS * HEAD_DIM), bf),
            pltpu.SMEM((BLOCK,), i32),
            pltpu.SemaphoreType.DMA((3,)),
        ],
    )(positions, jnp.asarray(inverse_row()), keys, values)
    chunks = lax.all_to_all(send.reshape(DEVICES, 8, HEAD_DIM), AXES, 0, 0, tiled=True)
    table = pl.BlockSpec((BLOCK, HEAD_DIM), lambda h: (0, 0))
    head = pl.BlockSpec((BLOCK, HEAD_DIM), lambda h: (0, h))
    picks, slots, count = pl.pallas_call(
        plan_kernel,
        out_shape=(
            jax.ShapeDtypeStruct((CAP, PLANES), i32),
            jax.ShapeDtypeStruct((8, ANC_MAX), i32),
            jax.ShapeDtypeStruct((1, 1), i32),
        ),
        in_specs=[VMEM, VMEM],
        compiler_params=room(8),
        cost_estimate=pl.CostEstimate(flops=4 << 20, bytes_accessed=4 << 20, transcendentals=0),
    )(token_block.reshape(DEVICES, BLOCK), ancestors.T)
    bundle = pl.pallas_call(
        bundle_kernel,
        grid=(KV_HEADS,),
        out_shape=jax.ShapeDtypeStruct((KV_HEADS, BLOCK, PACK), bf),
        in_specs=[VMEM_ONE, table, table, pl.BlockSpec((BLOCK, GROUP * HEAD_DIM), lambda h: (0, h)), head, head],
        out_specs=pl.BlockSpec((None, BLOCK, PACK), lambda h: (h, 0, 0)),
        compiler_params=room(8),
        cost_estimate=pl.CostEstimate(flops=4 << 20, bytes_accessed=4 << 20, transcendentals=0),
    )(count, cosine, sine, queries, own_k, values)
    members = lax.all_to_all(bundle, HEAD_AXES, 0, 0, tiled=True)
    fits = count[0, 0] <= CAP
    outs = quick(picks, slots, chunks, members)
    return lax.cond(fits, join, general, outs, chunks, bundle, token_block, ancestors)


def solution(mesh):
    fine = Mesh(mesh.devices.reshape(8, 2, 4, 2, 2), AXES)
    rows = P(AXES, None)

    return jax.shard_map(
        shards,
        mesh=fine,
        in_specs=(rows, rows, rows, P(), P(), P()),
        out_specs=rows,
        check_vma=False,
    )
```

profile of v0, /device:TPU:4, one launch (start us, length us, event | category | flops | bytes accessed | tf_op | source)
XLA Modules:
  0.0 105.2 jit_solution(18141130516203474526)
XLA Ops:
  0.0 2.8 %shard_map.76 = (bf16[8,2,4,2,2,8,128]{6,5,4,3,2,1,0:T(8,128)(2,1)}, f32[128,128]{1,0:T(8,128)}, f32[128,128]{1,0:T(8,128)}, bf16[128,1024]{1,0:T(8,128)(2,1)}) custom-call(s32[32768]{0:T(1024)} %pos_ref.1, f32[1,128]{1,0:T(1,128)} %constant.46.clone.inv_ref, bf16[128,1024]{1,0:T(8,128)(2,1)} %k_hbm.1, bf16[128,1024]{1,0:T(8,128)(2,1)} %v_ref.1), custom_call_target="tpu_custom_call" | custom-call | tf_op jit(solution)/shard_map/pallas_call | solution.py:358
  2.8 14.7 %all-to-all-start.1 = ((bf16[256,8,128]{2,1,0:T(8,128)(2,1)}), bf16[256,8,128]{2,1,0:T(8,128)(2,1)S(1)}, u32[]{:S(2)}, u32[]{:S(2)}) async-start(bf16[256,8,128]{2,1,0:T(8,128)(2,1)} %bitcast.26), calls=%async_computation.1 | async-start | bytes 1048576 | tf_op jit(solution)/shard_map/all_to_all | solution.py:373
  17.5 2.1 %shard_map.75 = (s32[34,8]{1,0:T(8,128)S(1)}, s32[8,8]{1,0:T(8,128)S(1)}, s32[1,1]{1,0:T(1,128)}) custom-call(s32[256,128]{1,0:T(8,128)} %bitcast.27, s32[8,256]{1,0:T(8,128)} %bitcast.36), custom_call_target="tpu_custom_call" | custom-call | flops 4194304 | bytes 4194304 | tf_op jit(solution)/shard_map/pallas_call | solution.py:376
  19.6 0.0 copy-start
  19.6 1.2 %copy-done = bf16[128,4096]{1,0:T(8,128)(2,1)S(1)} copy-done((bf16[128,4096]{1,0:T(8,128)(2,1)S(1)}, bf16[128,4096]{1,0:T(8,128)(2,1)}, u32[]{:S(2)}) %copy-start) | copy-done | bytes 1048600
  20.8 0.0 copy-start.1
  20.8 0.9 copy-done.1
  21.8 0.0 copy-start.2
  21.8 0.9 copy-done.2
  22.7 0.0 copy-start.3
  22.7 0.8 copy-done.3
  23.6 0.8 copy-done.4
  24.4 4.2 %shard_map.77 = bf16[8,128,768]{2,1,0:T(8,128)(2,1)} custom-call(s32[1,1]{1,0:T(1,128)} %get-tuple-element.67.count_ref, f32[128,128]{1,0:T(8,128)S(1)} %copy-done.3, f32[128,128]{1,0:T(8,128)S(1)} %copy-done.4, bf16[128,4096]{1,0:T(8,128)(2,1)S(1)} %copy-done, bf16[128,1024]{1,0:T(8,128)(2,1)S(1)} %copy-done.2, bf16[128,1024]{1,0:T(8,128)(2,1)S(1)} %copy-done.1), custom_call_target="tpu_custom_call" | custom-call | flops 4194304 | bytes 4194304 | tf_op jit(solution)/shard_map/pallas_call | solution.py:387
  28.6 8.6 %all-to-all-done.1.src_ref = bf16[256,8,128]{2,1,0:T(8,128)(2,1)S(1)} async-done(((bf16[256,8,128]{2,1,0:T(8,128)(2,1)}), bf16[256,8,128]{2,1,0:T(8,128)(2,1)S(1)}, u32[]{:S(2)}, u32[]{:S(2)}) %all-to-all-start.1) | async-done | bytes 524320 | tf_op jit(solution)/shard_map/all_to_all | solution.py:373
  37.2 3.6 %all-to-all-start.2 = ((bf16[8,128,768]{2,1,0:T(8,128)(2,1)}), bf16[8,128,768]{2,1,0:T(8,128)(2,1)S(1)}, u32[]{:S(2)}, u32[]{:S(2)}) async-start(bf16[8,128,768]{2,1,0:T(8,128)(2,1)} %shard_map.77), calls=%async_computation.2 | async-start | bytes 3145728 | tf_op jit(solution)/shard_map/all_to_all | solution.py:396
  40.8 1.3 %shard_map.78 = (bf16[34,8,128]{2,1,0:T(8,128)(2,1)S(1)}, bf16[34,8,128]{2,1,0:T(8,128)(2,1)S(1)}, bf16[34,8,128]{2,1,0:T(8,128)(2,1)S(1)}, bf16[34,8,128]{2,1,0...) custom-call(s32[34,8]{1,0:T(8,128)S(1)} %get-tuple-element.73.picks_, ...), custom_call_target="tpu_custom_call" | custom-call | tf_op jit(solution)/shard_map/pallas_call | solution.py:272
  42.1 0.1 collective-permute-start.3
  42.2 3.4 %collective-permute-start.4 = (bf16[34,8,128]{2,1,0:T(8,128)(2,1)S(1)}, bf16[34,8,128]{2,1,0:T(8,128)(2,1)S(1)}, u32[]{:S(2)}, u32[]{:S(2)}) collective-permute-start(bf16[34,8,128]{2,1,0:T(8,128)(2,1)S(1)} %get-tuple-element.79), channel_id=1, source_target_pairs={{0,96},{32,128},{64,160},{96,192},{128,224},{160,0},{192,32},{224,... | collective-permute-start | bytes 208904 | tf_op jit(solution)/shard_map/ppermute | solution.py:284
  45.6 1.7 %collective-permute-start.5 = (bf16[34,8,128]{2,1,0:T(8,128)(2,1)S(1)}, bf16[34,8,128]{2,1,0:T(8,128)(2,1)S(1)}, u32[]{:S(2)}, u32[]{:S(2)}) collective-permute-start(bf16[34,8,128]{2,1,0:T(8,128)(2,1)S(1)} %get-tuple-element.80), channel_id=1, source_target_pairs={{0,160},{32,192},{64,224},{96,0},{128,32},{160,64},{192,96},{224,1... | collective-permute-start | bytes 208904 | tf_op jit(solution)/shard_map/ppermute | solution.py:284
  47.3 4.2 %collective-permute-start.6 = (bf16[34,8,128]{2,1,0:T(8,128)(2,1)S(1)}, bf16[34,8,128]{2,1,0:T(8,128)(2,1)S(1)}, u32[]{:S(2)}, u32[]{:S(2)}) collective-permute-start(bf16[34,8,128]{2,1,0:T(8,128)(2,1)S(1)} %get-tuple-element.81), channel_id=1, source_target_pairs={{0,128},{32,160},{64,192},{96,224},{128,0},{160,32},{192,64},{224,... | collective-permute-start | bytes 208904 | tf_op jit(solution)/shard_map/ppermute | solution.py:284
  51.5 0.6 collective-permute-start
  52.0 0.0 collective-permute-done.3
  52.0 2.7 %collective-permute-start.1 = (bf16[34,8,128]{2,1,0:T(8,128)(2,1)S(1)}, bf16[34,8,128]{2,1,0:T(8,128)(2,1)S(1)}, u32[]{:S(2)}, u32[]{:S(2)}) collective-permute-start(bf16[34,8,128]{2,1,0:T(8,128)(2,1)S(1)} %get-tuple-element.76), channel_id=1, source_target_pairs={{0,224},{32,0},{64,32},{96,64},{128,96},{160,128},{192,160},{224,1... | collective-permute-start | bytes 208904 | tf_op jit(solution)/shard_map/ppermute | solution.py:284
  54.7 0.0 collective-permute-done.4
  54.7 0.0 collective-permute-start.2
  54.7 0.2 collective-permute-done.5
  54.9 2.1 %collective-permute-done.6 = bf16[34,8,128]{2,1,0:T(8,128)(2,1)S(1)} collective-permute-done((bf16[34,8,128]{2,1,0:T(8,128)(2,1)S(1)}, bf16[34,8,128]{2,1,0:T(8,128)(2,1)S(1)}, u32[]{:S(2)}, u32[]{:S(2)}) %collective-permute-start.6) | collective-permute-done | bytes 69664 | tf_op jit(solution)/shard_map/ppermute | solution.py:284
  57.0 0.0 copy-done.5
  57.0 2.3 %collective-permute-start.8 = (bf16[34,32,128]{2,1,0:T(8,128)(2,1)S(1)}, bf16[34,32,128]{2,1,0:T(8,128)(2,1)S(1)}, u32[]{:S(2)}, u32[]{:S(2)}) collective-permute-start(bf16[34,32,128]{2,1,0:T(8,128)(2,1)S(1)} %copy_bitcast_fusion.refs_1_), channel_id=1, source_target_pairs={{0,2},{2,0},{1,3},{3,1},{4,6},{6,4},{5,7},{7,5},{8,10},{10,8},{9,1... | collective-permute-start | bytes 835592 | tf_op jit(solution)/shard_map/ppermute | solution.py:291
  59.3 0.0 collective-permute-done
  59.3 0.0 collective-permute-done.1
  59.3 1.9 %collective-permute-done.2 = bf16[34,8,128]{2,1,0:T(8,128)(2,1)S(1)} collective-permute-done((bf16[34,8,128]{2,1,0:T(8,128)(2,1)S(1)}, bf16[34,8,128]{2,1,0:T(8,128)(2,1)S(1)}, u32[]{:S(2)}, u32[]{:S(2)}) %collective-permute-start.2) | collective-permute-done | bytes 69664 | tf_op jit(solution)/shard_map/ppermute | solution.py:284
  61.3 2.0 %collective-permute-start.7 = (bf16[34,32,128]{2,1,0:T(8,128)(2,1)S(1)}, bf16[34,32,128]{2,1,0:T(8,128)(2,1)S(1)}, u32[]{:S(2)}, u32[]{:S(2)}) collective-permute-start(bf16[34,32,128]{2,1,0:T(8,128)(2,1)S(1)} %copy_bitcast_fusion.1.refs_0_), channel_id=1, source_target_pairs={{0,2},{2,0},{1,3},{3,1},{4,6},{6,4},{5,7},{7,5},{8,10},{10,8},{9,1... | collective-permute-start | bytes 835592 | tf_op jit(solution)/shard_map/ppermute | solution.py:291
  63.3 0.0 collective-permute-start.10
  63.3 0.5 collective-permute-start.9
  63.8 4.4 %collective-permute-done.8.refs_3_ = bf16[34,32,128]{2,1,0:T(8,128)(2,1)S(1)} collective-permute-done((bf16[34,32,128]{2,1,0:T(8,128)(2,1)S(1)}, bf16[34,32,128]{2,1,0:T(8,128)(2,1)S(1)}, u32[]{:S(2)}, u32[]{:S(2)}) %collective-permute-start.8) | collective-permute-done | bytes 278560 | tf_op jit(solution)/shard_map/ppermute | solution.py:291
  68.2 0.0 collective-permute-start.12
  68.2 4.3 %collective-permute-done.7.refs_2_ = bf16[34,32,128]{2,1,0:T(8,128)(2,1)S(1)} collective-permute-done((bf16[34,32,128]{2,1,0:T(8,128)(2,1)S(1)}, bf16[34,32,128]{2,1,0:T(8,128)(2,1)S(1)}, u32[]{:S(2)}, u32[]{:S(2)}) %collective-permute-start.7) | collective-permute-done | bytes 278560 | tf_op jit(solution)/shard_map/ppermute | solution.py:291
  72.4 0.0 collective-permute-start.11
  72.4 0.0 all-to-all-done.2.x_ref
  72.4 0.0 collective-permute-done.10.refs_5_
  72.5 0.0 collective-permute-done.9.refs_4_
  72.5 0.0 collective-permute-done.12.refs_7_
  72.5 1.7 %collective-permute-done.11.refs_6_ = bf16[34,32,128]{2,1,0:T(8,128)(2,1)} collective-permute-done((bf16[34,32,128]{2,1,0:T(8,128)(2,1)S(1)}, bf16[34,32,128]{2,1,0:T(8,128)(2,1)}, u32[]{:S(2)}, u32[]{:S(2)}) %collective-permute-start.11) | collective-permute-done | bytes 278560 | tf_op jit(solution)/shard_map/ppermute | solution.py:294
  74.1 5.1 %shard_map.80 = (bf16[128,512]{1,0:T(8,128)(2,1)S(1)}, bf16[128,512]{1,0:T(8,128)(2,1)S(1)}, bf16[128,512]{1,0:T(8,128)(2,1)S(1)}, bf16[128,512]{1,0:T(8,128)(2,1)S(1)}) custom-call(s32[8,8]{1,0:T(8,128)S(1)} %get-tuple-element.72.slots_ref, bf16[8,128,768]{2,1,0:T(8,128)(2,1)S(1)} %all-to-all-done.2.x_ref, ...), custom_call_target="tpu_custom_call" | custom-call | flops 1073741824 | bytes 2097152 | tf_op jit(solution)/shard_map/pallas_call | solution.py:298
  79.2 3.1 %collective-permute-start.16 = (bf16[128,512]{1,0:T(8,128)(2,1)S(1)}, bf16[128,512]{1,0:T(8,128)(2,1)}, u32[]{:S(2)}, u32[]{:S(2)}) collective-permute-start(bf16[128,512]{1,0:T(8,128)(2,1)S(1)} %get-tuple-element.86), channel_id=1, source_target_pairs={{0,8},{1,9},{4,12},{5,13},{8,0},{9,1},{12,4},{13,5},{2,10},{3,11},... | collective-permute-start | bytes 393224 | tf_op jit(solution)/shard_map/ppermute | solution.py:312
  82.4 2.9 %collective-permute-start.17 = (bf16[128,512]{1,0:T(8,128)(2,1)S(1)}, bf16[128,512]{1,0:T(8,128)(2,1)}, u32[]{:S(2)}, u32[]{:S(2)}) collective-permute-start(bf16[128,512]{1,0:T(8,128)(2,1)S(1)} %get-tuple-element.87), channel_id=1, source_target_pairs={{0,9},{1,8},{4,13},{5,12},{8,1},{9,0},{12,5},{13,4},{2,11},{3,10},... | collective-permute-start | bytes 393224 | tf_op jit(solution)/shard_map/ppermute | solution.py:312
  85.3 1.8 %collective-permute-start.18 = (bf16[128,512]{1,0:T(8,128)(2,1)S(1)}, bf16[128,512]{1,0:T(8,128)(2,1)}, u32[]{:S(2)}, u32[]{:S(2)}) collective-permute-start(bf16[128,512]{1,0:T(8,128)(2,1)S(1)} %get-tuple-element.88), channel_id=1, source_target_pairs={{0,12},{1,13},{4,8},{5,9},{8,4},{9,5},{12,0},{13,1},{2,14},{3,15},... | collective-permute-start | bytes 393224 | tf_op jit(solution)/shard_map/ppermute | solution.py:312
  87.1 0.6 collective-permute-start.19
  87.7 5.7 %shard_map.79 = (bf16[128,512]{1,0:T(8,128)(2,1)}, bf16[128,512]{1,0:T(8,128)(2,1)S(1)}, bf16[128,512]{1,0:T(8,128)(2,1)S(1)}, bf16[128,512]{1,0:T(8,128)(2,1)S(1)}) custom-call(s32[8,8]{1,0:T(8,128)S(1)} %get-tuple-element.72.slots_ref, bf16[8,128,768]{2,1,0:T(8,128)(2,1)S(1)} %all-to-all-done.2.x_ref, bf16[34,32,128]{2,1,0:T(8,128)(2,1)S(1)} %copy_bitcast_fusion.1.refs_0_, ...), custom_call_target="tpu_custom_call" | custom-call | flops 1073741824 | bytes 2097152 | tf_op jit(solution)/shard_map/pallas_call | solution.py:298
  93.4 2.3 %collective-permute-start.13 = (bf16[128,512]{1,0:T(8,128)(2,1)S(1)}, bf16[128,512]{1,0:T(8,128)(2,1)}, u32[]{:S(2)}, u32[]{:S(2)}) collective-permute-start(bf16[128,512]{1,0:T(8,128)(2,1)S(1)} %get-tuple-element.83), channel_id=1, source_target_pairs={{0,1},{1,0},{4,5},{5,4},{8,9},{9,8},{12,13},{13,12},{2,3},{3,2},{6... | collective-permute-start | bytes 393224 | tf_op jit(solution)/shard_map/ppermute | solution.py:312
  95.7 0.0 collective-permute-done.16
  95.7 0.0 collective-permute-start.14
  95.7 0.0 collective-permute-done.17
  95.7 1.5 %collective-permute-start.15 = (bf16[128,512]{1,0:T(8,128)(2,1)S(1)}, bf16[128,512]{1,0:T(8,128)(2,1)}, u32[]{:S(2)}, u32[]{:S(2)}) collective-permute-start(bf16[128,512]{1,0:T(8,128)(2,1)S(1)} %get-tuple-element.85), channel_id=1, source_target_pairs={{0,5},{1,4},{4,1},{5,0},{8,13},{9,12},{12,9},{13,8},{2,7},{3,6},{6... | collective-permute-start | bytes 393224 | tf_op jit(solution)/shard_map/ppermute | solution.py:312
  97.8 0.0 collective-permute-done.18
  97.8 0.0 collective-permute-done.19
  97.8 1.4 %collective-permute-done.13 = bf16[128,512]{1,0:T(8,128)(2,1)} collective-permute-done((bf16[128,512]{1,0:T(8,128)(2,1)S(1)}, bf16[128,512]{1,0:T(8,128)(2,1)}, u32[]{:S(2)}, u32[]{:S(2)}) %collective-permute-start.13) | collective-permute-done | bytes 131104 | tf_op jit(solution)/shard_map/ppermute | solution.py:312
  99.1 3.6 %collective-permute-done.14 = bf16[128,512]{1,0:T(8,128)(2,1)} collective-permute-done((bf16[128,512]{1,0:T(8,128)(2,1)S(1)}, bf16[128,512]{1,0:T(8,128)(2,1)}, u32[]{:S(2)}, u32[]{:S(2)}) %collective-permute-start.14) | collective-permute-done | bytes 131104 | tf_op jit(solution)/shard_map/ppermute | solution.py:312
  102.7 0.0 collective-permute-done.15
  102.7 0.0 copy-done.7
  102.7 0.0 copy-done.8
  102.7 2.3 %conditional.1 = (bf16[128,4096]{1,0:T(8,128)(2,1)}) conditional(s32[]{:T(128)} %bitcast.8, (s32[32768]{0:T(1024)S(1)}, s32[256,8]{0,1:T(8,128)S(1)}, bf16[256,8,128]{2,1,0:T(8,128)(2,1)}, bf16[8,128,768]{2,1,0:T(8,128)(2,1)}) %tuple.25, (bf16[128,512]{1,0:T(8,128)(2,1)}, bf16[128,512]{1,0:T(8,128)(2,1)}, bf16[128,512]{1,0:T(8,128)(2,1)}, ...), branch_computations={%region_0.3_spmd, %region_3.4_spmd} | conditional | flops 208409 | bytes 20584806 | solution.py:399
  102.7 2.3 %branch_1_fun.1 = bf16[128,4096]{1,0:T(8,128)(2,1)} custom-call(bf16[128,512]{1,0:T(8,128)(2,1)} %get-tuple-element.36.refs_0_, bf16[128,512]{1,0:T(8,128)(2,1)} %get-tuple-element.37.refs_1_, bf16[128,512]{1,0:T(8,128)(2,1)} %get-tuple-element.38.refs_2_, bf16[128,512]{1,0:T(8,128)(2,1)} %get-tuple-element.39.refs_3_, ...), custom_call_target="tpu_custom_call" | custom-call | tf_op jit(solution)/shard_map/cond/branch_1_fun/pallas_call | solution.py:317
  (6 shorter events, 0.1 us)
Async XLA Ops:
  2.8 34.4 %all-to-all-start.1 = ((bf16[256,8,128]{2,1,0:T(8,128)(2,1)}), bf16[256,8,128]{2,1,0:T(8,128)(2,1)S(1)}, u32[]{:S(2)}, u32[]{:S(2)}) async-start(bf16[256,8,128]{2,1,0:T(8,128)(2,1)} %bitcast.26), calls=%async_computation.1 | async-start | bytes 1048576 | tf_op jit(solution)/shard_map/all_to_all | solution.py:373
  19.6 1.2 %copy-start = (bf16[128,4096]{1,0:T(8,128)(2,1)S(1)}, bf16[128,4096]{1,0:T(8,128)(2,1)}, u32[]{:S(2)}) copy-start(bf16[128,4096]{1,0:T(8,128)(2,1)} %q_ref.1) | copy-start | bytes 3145732
  20.8 0.9 copy-start.1
  21.8 0.9 copy-start.2
  22.7 0.8 copy-start.3
  23.6 0.8 copy-start.4
  37.2 19.8 %copy-start.5 = (bf16[256,8,128]{2,1,0:T(8,128)(2,1)}, bf16[256,8,128]{2,1,0:T(8,128)(2,1)S(1)}, u32[]{:S(2)}) copy-start(bf16[256,8,128]{2,1,0:T(8,128)(2,1)S(1)} %all-to-all-done.1.src_ref) | copy-start | bytes 1572868
  37.2 35.2 %all-to-all-start.2 = ((bf16[8,128,768]{2,1,0:T(8,128)(2,1)}), bf16[8,128,768]{2,1,0:T(8,128)(2,1)S(1)}, u32[]{:S(2)}, u32[]{:S(2)}) async-start(bf16[8,128,768]{2,1,0:T(8,128)(2,1)} %shard_map.77), calls=%async_computation.2 | async-start | bytes 3145728 | tf_op jit(solution)/shard_map/all_to_all | solution.py:396
  42.1 10.0 %collective-permute-start.3 = (bf16[34,8,128]{2,1,0:T(8,128)(2,1)S(1)}, bf16[34,8,128]{2,1,0:T(8,128)(2,1)S(1)}, u32[]{:S(2)}, u32[]{:S(2)}) collective-permute-start(bf16[34,8,128]{2,1,0:T(8,128)(2,1)S(1)} %get-tuple-element.78), channel_id=1, source_target_pairs={{0,192},{32,224},{64,0},{96,32},{128,64},{160,96},{192,128},{224,1... | collective-permute-start | bytes 208904 | tf_op jit(solution)/shard_map/ppermute | solution.py:284
  42.2 12.5 %collective-permute-start.4 = (bf16[34,8,128]{2,1,0:T(8,128)(2,1)S(1)}, bf16[34,8,128]{2,1,0:T(8,128)(2,1)S(1)}, u32[]{:S(2)}, u32[]{:S(2)}) collective-permute-start(bf16[34,8,128]{2,1,0:T(8,128)(2,1)S(1)} %get-tuple-element.79), channel_id=1, source_target_pairs={{0,96},{32,128},{64,160},{96,192},{128,224},{160,0},{192,32},{224,... | collective-permute-start | bytes 208904 | tf_op jit(solution)/shard_map/ppermute | solution.py:284
  45.6 9.3 %collective-permute-start.5 = (bf16[34,8,128]{2,1,0:T(8,128)(2,1)S(1)}, bf16[34,8,128]{2,1,0:T(8,128)(2,1)S(1)}, u32[]{:S(2)}, u32[]{:S(2)}) collective-permute-start(bf16[34,8,128]{2,1,0:T(8,128)(2,1)S(1)} %get-tuple-element.80), channel_id=1, source_target_pairs={{0,160},{32,192},{64,224},{96,0},{128,32},{160,64},{192,96},{224,1... | collective-permute-start | bytes 208904 | tf_op jit(solution)/shard_map/ppermute | solution.py:284
  47.3 9.7 %collective-permute-start.6 = (bf16[34,8,128]{2,1,0:T(8,128)(2,1)S(1)}, bf16[34,8,128]{2,1,0:T(8,128)(2,1)S(1)}, u32[]{:S(2)}, u32[]{:S(2)}) collective-permute-start(bf16[34,8,128]{2,1,0:T(8,128)(2,1)S(1)} %get-tuple-element.81), channel_id=1, source_target_pairs={{0,128},{32,160},{64,192},{96,224},{128,0},{160,32},{192,64},{224,... | collective-permute-start | bytes 208904 | tf_op jit(solution)/shard_map/ppermute | solution.py:284
  51.5 7.9 %collective-permute-start = (bf16[34,8,128]{2,1,0:T(8,128)(2,1)S(1)}, bf16[34,8,128]{2,1,0:T(8,128)(2,1)S(1)}, u32[]{:S(2)}, u32[]{:S(2)}) collective-permute-start(bf16[34,8,128]{2,1,0:T(8,128)(2,1)S(1)} %get-tuple-element.75), channel_id=1, source_target_pairs={{0,32},{32,64},{64,96},{96,128},{128,160},{160,192},{192,224},{224... | collective-permute-start | bytes 208904 | tf_op jit(solution)/shard_map/ppermute | solution.py:284
  52.0 7.3 %collective-permute-start.1 = (bf16[34,8,128]{2,1,0:T(8,128)(2,1)S(1)}, bf16[34,8,128]{2,1,0:T(8,128)(2,1)S(1)}, u32[]{:S(2)}, u32[]{:S(2)}) collective-permute-start(bf16[34,8,128]{2,1,0:T(8,128)(2,1)S(1)} %get-tuple-element.76), channel_id=1, source_target_pairs={{0,224},{32,0},{64,32},{96,64},{128,96},{160,128},{192,160},{224,1... | collective-permute-start | bytes 208904 | tf_op jit(solution)/shard_map/ppermute | solution.py:284
  54.7 6.6 %collective-permute-start.2 = (bf16[34,8,128]{2,1,0:T(8,128)(2,1)S(1)}, bf16[34,8,128]{2,1,0:T(8,128)(2,1)S(1)}, u32[]{:S(2)}, u32[]{:S(2)}) collective-permute-start(bf16[34,8,128]{2,1,0:T(8,128)(2,1)S(1)} %get-tuple-element.77), channel_id=1, source_target_pairs={{0,64},{32,96},{64,128},{96,160},{128,192},{160,224},{192,0},{224,... | collective-permute-start | bytes 208904 | tf_op jit(solution)/shard_map/ppermute | solution.py:284
  57.0 11.1 %collective-permute-start.8 = (bf16[34,32,128]{2,1,0:T(8,128)(2,1)S(1)}, bf16[34,32,128]{2,1,0:T(8,128)(2,1)S(1)}, u32[]{:S(2)}, u32[]{:S(2)}) collective-permute-start(bf16[34,32,128]{2,1,0:T(8,128)(2,1)S(1)} %copy_bitcast_fusion.refs_1_), channel_id=1, source_target_pairs={{0,2},{2,0},{1,3},{3,1},{4,6},{6,4},{5,7},{7,5},{8,10},{10,8},{9,1... | collective-permute-start | bytes 835592 | tf_op jit(solution)/shard_map/ppermute | solution.py:291
  61.3 11.1 %collective-permute-start.7 = (bf16[34,32,128]{2,1,0:T(8,128)(2,1)S(1)}, bf16[34,32,128]{2,1,0:T(8,128)(2,1)S(1)}, u32[]{:S(2)}, u32[]{:S(2)}) collective-permute-start(bf16[34,32,128]{2,1,0:T(8,128)(2,1)S(1)} %copy_bitcast_fusion.1.refs_0_), channel_id=1, source_target_pairs={{0,2},{2,0},{1,3},{3,1},{4,6},{6,4},{5,7},{7,5},{8,10},{10,8},{9,1... | collective-permute-start | bytes 835592 | tf_op jit(solution)/shard_map/ppermute | solution.py:291
  63.3 9.2 %collective-permute-start.10 = (bf16[34,32,128]{2,1,0:T(8,128)(2,1)S(1)}, bf16[34,32,128]{2,1,0:T(8,128)(2,1)S(1)}, u32[]{:S(2)}, u32[]{:S(2)}) collective-permute-start(bf16[34,32,128]{2,1,0:T(8,128)(2,1)S(1)} %copy_bitcast_fusion.refs_1_), channel_id=1, source_target_pairs={{0,16},{16,0},{1,17},{17,1},{2,18},{18,2},{3,19},{19,3},{4,20},{20... | collective-permute-start | bytes 835592 | tf_op jit(solution)/shard_map/ppermute | solution.py:292
  63.3 9.2 %collective-permute-start.9 = (bf16[34,32,128]{2,1,0:T(8,128)(2,1)S(1)}, bf16[34,32,128]{2,1,0:T(8,128)(2,1)S(1)}, u32[]{:S(2)}, u32[]{:S(2)}) collective-permute-start(bf16[34,32,128]{2,1,0:T(8,128)(2,1)S(1)} %copy_bitcast_fusion.1.refs_0_), channel_id=1, source_target_pairs={{0,16},{16,0},{1,17},{17,1},{2,18},{18,2},{3,19},{19,3},{4,20},{20... | collective-permute-start | bytes 835592 | tf_op jit(solution)/shard_map/ppermute | solution.py:292
  68.2 4.3 %collective-permute-start.12 = (bf16[34,32,128]{2,1,0:T(8,128)(2,1)S(1)}, bf16[34,32,128]{2,1,0:T(8,128)(2,1)S(1)}, u32[]{:S(2)}, u32[]{:S(2)}) collective-permute-start(bf16[34,32,128]{2,1,0:T(8,128)(2,1)S(1)} %collective-permute-done.8.refs_3_), channel_id=1, source_target_pairs={{0,16},{16,0},{1,17},{17,1},{2,18},{18,2},{3,19},{19,3},{4,20},{20... | collective-permute-start | bytes 835592 | tf_op jit(solution)/shard_map/ppermute | solution.py:294
  72.4 1.7 %collective-permute-start.11 = (bf16[34,32,128]{2,1,0:T(8,128)(2,1)S(1)}, bf16[34,32,128]{2,1,0:T(8,128)(2,1)}, u32[]{:S(2)}, u32[]{:S(2)}) collective-permute-start(bf16[34,32,128]{2,1,0:T(8,128)(2,1)S(1)} %collective-permute-done.7.refs_2_), channel_id=1, source_target_pairs={{0,16},{16,0},{1,17},{17,1},{2,18},{18,2},{3,19},{19,3},{4,20},{20... | collective-permute-start | bytes 835592 | tf_op jit(solution)/shard_map/ppermute | solution.py:294
  74.1 28.6 %copy-start.7 = (s32[32768]{0:T(1024)S(1)}, s32[32768]{0:T(1024)}, u32[]{:S(2)}) copy-start(s32[32768]{0:T(1024)} %param.13) | copy-start | bytes 393220
  74.1 28.6 %copy-start.8 = (s32[256,8]{0,1:T(8,128)S(1)}, s32[256,8]{0,1:T(8,128)}, u32[]{:S(2)}) copy-start(s32[256,8]{0,1:T(8,128)} %param.12) | copy-start | bytes 24580
  79.2 16.4 %collective-permute-start.16 = (bf16[128,512]{1,0:T(8,128)(2,1)S(1)}, bf16[128,512]{1,0:T(8,128)(2,1)}, u32[]{:S(2)}, u32[]{:S(2)}) collective-permute-start(bf16[128,512]{1,0:T(8,128)(2,1)S(1)} %get-tuple-element.86), channel_id=1, source_target_pairs={{0,8},{1,9},{4,12},{5,13},{8,0},{9,1},{12,4},{13,5},{2,10},{3,11},... | collective-permute-start | bytes 393224 | tf_op jit(solution)/shard_map/ppermute | solution.py:312
  82.4 13.3 %collective-permute-start.17 = (bf16[128,512]{1,0:T(8,128)(2,1)S(1)}, bf16[128,512]{1,0:T(8,128)(2,1)}, u32[]{:S(2)}, u32[]{:S(2)}) collective-permute-start(bf16[128,512]{1,0:T(8,128)(2,1)S(1)} %get-tuple-element.87), channel_id=1, source_target_pairs={{0,9},{1,8},{4,13},{5,12},{8,1},{9,0},{12,5},{13,4},{2,11},{3,10},... | collective-permute-start | bytes 393224 | tf_op jit(solution)/shard_map/ppermute | solution.py:312
  85.3 12.5 %collective-permute-start.18 = (bf16[128,512]{1,0:T(8,128)(2,1)S(1)}, bf16[128,512]{1,0:T(8,128)(2,1)}, u32[]{:S(2)}, u32[]{:S(2)}) collective-permute-start(bf16[128,512]{1,0:T(8,128)(2,1)S(1)} %get-tuple-element.88), channel_id=1, source_target_pairs={{0,12},{1,13},{4,8},{5,9},{8,4},{9,5},{12,0},{13,1},{2,14},{3,15},... | collective-permute-start | bytes 393224 | tf_op jit(solution)/shard_map/ppermute | solution.py:312
  87.1 10.7 %collective-permute-start.19 = (bf16[128,512]{1,0:T(8,128)(2,1)S(1)}, bf16[128,512]{1,0:T(8,128)(2,1)}, u32[]{:S(2)}, u32[]{:S(2)}) collective-permute-start(bf16[128,512]{1,0:T(8,128)(2,1)S(1)} %get-tuple-element.89), channel_id=1, source_target_pairs={{0,13},{1,12},{4,9},{5,8},{8,5},{9,4},{12,1},{13,0},{2,15},{3,14},... | collective-permute-start | bytes 393224 | tf_op jit(solution)/shard_map/ppermute | solution.py:312
  93.4 5.8 %collective-permute-start.13 = (bf16[128,512]{1,0:T(8,128)(2,1)S(1)}, bf16[128,512]{1,0:T(8,128)(2,1)}, u32[]{:S(2)}, u32[]{:S(2)}) collective-permute-start(bf16[128,512]{1,0:T(8,128)(2,1)S(1)} %get-tuple-element.83), channel_id=1, source_target_pairs={{0,1},{1,0},{4,5},{5,4},{8,9},{9,8},{12,13},{13,12},{2,3},{3,2},{6... | collective-permute-start | bytes 393224 | tf_op jit(solution)/shard_map/ppermute | solution.py:312
  95.7 7.0 %collective-permute-start.14 = (bf16[128,512]{1,0:T(8,128)(2,1)S(1)}, bf16[128,512]{1,0:T(8,128)(2,1)}, u32[]{:S(2)}, u32[]{:S(2)}) collective-permute-start(bf16[128,512]{1,0:T(8,128)(2,1)S(1)} %get-tuple-element.84), channel_id=1, source_target_pairs={{0,4},{1,5},{4,0},{5,1},{8,12},{9,13},{12,8},{13,9},{2,6},{3,7},{6... | collective-permute-start | bytes 393224 | tf_op jit(solution)/shard_map/ppermute | solution.py:312
  95.7 7.0 %collective-permute-start.15 = (bf16[128,512]{1,0:T(8,128)(2,1)S(1)}, bf16[128,512]{1,0:T(8,128)(2,1)}, u32[]{:S(2)}, u32[]{:S(2)}) collective-permute-start(bf16[128,512]{1,0:T(8,128)(2,1)S(1)} %get-tuple-element.85), channel_id=1, source_target_pairs={{0,5},{1,4},{4,1},{5,0},{8,13},{9,12},{12,9},{13,8},{2,7},{3,6},{6... | collective-permute-start | bytes 393224 | tf_op jit(solution)/shard_map/ppermute | solution.py:312
where the time goes:
time: 106 us; the launch traced here: 105 us
  starting transfers between devices  47.9 us (45%)
  waiting for transfers between devices  28.1 us (27%)
  Pallas kernels  23.4 us (22%)
  local copies, waits for them, and re-layouts  4.81 us (5%)
    all_to_all x1, starting transfers between devices, shards(): lax.all_to_all(send.reshape(DEVICES, 8, HEAD_DIM), AXES, 0, 0, tiled=True)  14.7 us
    ppermute x7, starting transfers between devices, quick(): got[d] = lax.ppermute(packs[d], 'z', pairs)  12.6 us
    ppermute x7, starting transfers between devices, quick(): outs[step] = lax.ppermute(out, HEAD_AXES, pairs) if step else out  12.2 us
    pallas_call x2, Pallas kernels, quick(): pl.pallas_call(functools.partial(span_kernel, mask), out_shape=[jax.Shape...  10.8 us
    ppermute x2, waiting for transfers between devices, quick(): far.append(lax.ppermute(part, 'xh', swap))  8.64 us
    all_to_all x1, waiting for transfers between devices, shards(): lax.all_to_all(send.reshape(DEVICES, 8, HEAD_DIM), AXES, 0, 0, tiled=True)  8.64 us
    ppermute x7, waiting for transfers between devices, quick(): outs[step] = lax.ppermute(out, HEAD_AXES, pairs) if step else out  4.94 us
    unnamed x16, local copies, waits for them, and re-layouts  4.81 us
  transfers between devices with their start and end apart: 22, of which 9 were waited for; matrix products, arithmetic and copies ran while one was open for 0% of the time, Pallas kernels for 13%

commit v1 on v0

--- a/solution.py
+++ b/solution.py
@@ -21,8 +21,8 @@
 PLANES = 8
 CAP = 34
 HALF = BLOCK // 2
-SHIFTS = ((0, 1, 7, 2), (6, 3, 5, 4))
-GROUPS = len(SHIFTS)
+REACH = 3
+GROUPS = 2
 KV_SCRATCH = [
     pltpu.VMEM((ANC_MAX * BLOCK, HEAD_DIM), jnp.bfloat16),
     pltpu.VMEM((ANC_MAX * BLOCK, 2 * HEAD_DIM), jnp.bfloat16),
@@ -153,13 +153,19 @@
     slots_ref[:, SLOTS:] = jnp.sum((path >= 0).astype(i32), axis=1, keepdims=True) - 1
 
 
-def pack_kernel(picks_ref, src_ref, *out_refs):
+def pack_kernel(picks_ref, src_ref, own_ref, mid_ref, keep_ref, give_ref):
     z = lax.axis_index("z")
-    for d in range(PLANES):
-        plane = lax.rem(z + d, PLANES)
+    side = 1 - 2 * lax.axis_index("c")
+    targets = [(own_ref, None, z), (mid_ref, None, z + PLANES // 2)]
+    for j in range(REACH):
+        targets.append((keep_ref, j, z + side * (j + 1)))
+        targets.append((give_ref, j, z - side * (j + 1)))
+    for out_ref, j, target in targets:
+        plane = lax.rem(target + PLANES, PLANES)
+        out_ref = out_ref if j is None else out_ref.at[j]
 
         def one(k, carry):
-            out_refs[d][k] = src_ref[picks_ref[k, plane]]
+            out_ref[k] = src_ref[picks_ref[k, plane]]
             return carry
 
         lax.fori_loop(0, CAP, one, 0, unroll=True)
@@ -206,36 +212,47 @@
     return lax.axis_index("y") * 2 + lax.axis_index("xl")
 
 
+SAME_KIND = ((0, 0, 0, 24, 0), (0, 1, 0, 16, 24), (1, 0, 24, 16, 40), (1, 1, 16, 8, 56))
+OTHER_KIND = (
+    (1, 0, 0, 8, 0),
+    (0, 0, 24, 16, 8),
+    (0, 1, 16, 8, 24),
+    (1, 1, 8, 8, 32),
+    (1, 0, 8, 16, 40),
+    (1, 1, 0, 8, 56),
+)
+
+
 def fill(k_ref, v_ref, slots_ref, m, here, there):
-    def copy(dst_ref, parts):
+    def copy(dst_ref, plan):
         for j in range(SLOTS):
             slot = slots_ref[m, j]
-            at = (j + 1) * BLOCK
-            for part in parts:
-                size = part.shape[1]
-                dst_ref[at : at + size, 0:HEAD_DIM] = part[slot]
-                at += size
+            for half in range(2):
+                at = (j + 1) * BLOCK + half * HALF
+                for other, group, row, rows, to in plan:
+                    part = (there if other else here)[half * GROUPS + group]
+                    dst_ref[at + to : at + to + rows, 0:HEAD_DIM] = part[slot, row : row + rows]
 
     core = lax.axis_index("c")
 
     @pl.when(core == 0)
     def _():
-        copy(k_ref, here)
-        copy(v_ref, there)
+        copy(k_ref, SAME_KIND)
+        copy(v_ref, OTHER_KIND)
 
     @pl.when(core != 0)
     def _():
-        copy(k_ref, there)
-        copy(v_ref, here)
-
-
-def span_kernel(mask, slots_ref, x_ref, *refs):
+        copy(k_ref, OTHER_KIND)
+        copy(v_ref, SAME_KIND)
+
+
+def span_kernel(first, slots_ref, x_ref, *refs):
     here, there = refs[: 2 * GROUPS], refs[2 * GROUPS : 4 * GROUPS]
     out_refs, (k_ref, v_ref, done_ref) = refs[4 * GROUPS : -3], refs[-3:]
     v_ref[:, HEAD_DIM:] = jnp.ones((ANC_MAX * BLOCK, HEAD_DIM), jnp.bfloat16)
 
     def one(n, carry):
-        m = own_member() ^ mask ^ n
+        m = own_member() ^ (n + first)
         fill(k_ref, v_ref, slots_ref, m, here, there)
         attention(x_ref.at[m], k_ref, v_ref, slots_ref[m, SLOTS], BLOCK, done_ref.at[n])
         return carry
@@ -253,38 +270,55 @@
 
 
 def join_kernel(*refs):
-    out_ref, sems = refs[-2], refs[-1]
+    out_ref, held_ref, sems = refs[-3:]
     width = GROUP * HEAD_DIM
-    copies = []
+    loads, stores = [], []
     for step in range(KV_HEADS):
         at = pl.multiple_of((own_member() ^ step) * width, width)
-        copies.append(
-            pltpu.make_async_copy(refs[step], out_ref.at[:, pl.ds(at, width)], sems.at[step])
-        )
-    for copy in copies:
-        copy.start()
-    for copy in copies:
-        copy.wait()
+        held = held_ref.at[step]
+        loads.append(pltpu.make_async_copy(refs[step], held, sems.at[0, step]))
+        stores.append(pltpu.make_async_copy(held, out_ref.at[:, pl.ds(at, width)], sems.at[1, step]))
+    for load in loads:
+        load.start()
+    for load, store in zip(loads, stores):
+        load.wait()
+        store.start()
+    for store in stores:
+        store.wait()
 
 
 def quick(picks, slots, chunks, members):
     bf = jnp.bfloat16
-    packs = pl.pallas_call(
+    piece = (CAP, 8, HEAD_DIM)
+    own, mid, keep, give = pl.pallas_call(
         pack_kernel,
-        out_shape=[jax.ShapeDtypeStruct((CAP, 8, HEAD_DIM), bf)] * PLANES,
+        out_shape=[
+            jax.ShapeDtypeStruct(piece, bf),
+            jax.ShapeDtypeStruct(piece, bf),
+            jax.ShapeDtypeStruct((REACH,) + piece, bf),
+            jax.ShapeDtypeStruct((REACH,) + piece, bf),
+        ],
         in_specs=[SMEM, VMEM],
         compiler_params=room(8),
     )(picks, chunks)
     swap = [(0, 1), (1, 0)]
-    got = {0: packs[0]}
-    for shifts in SHIFTS:
-        for d in shifts:
-            if d:
-                pairs = [(i, (i + d) % PLANES) for i in range(PLANES)]
-                got[d] = lax.ppermute(packs[d], "z", pairs)
+    taken = lax.ppermute(give, "c", swap)
+    mid = lax.ppermute(mid, "z", [(i, (i + 4) % PLANES) for i in range(PLANES)])
+    came = []
+    for j in range(REACH):
+        pairs = [
+            (z * 2 + c, (z + (1 - 2 * c) * (j + 1)) % PLANES * 2 + c)
+            for z in range(PLANES)
+            for c in range(2)
+        ]
+        came.append(lax.ppermute(jnp.stack([keep[j], taken[j]]), ("z", "c"), pairs))
+
+    def rows(parts):
+        return jnp.stack(parts, axis=1).reshape(CAP, 8 * len(parts), HEAD_DIM)
+
     near = [
-        jnp.stack([got[d] for d in shifts], axis=1).reshape(CAP, 8 * len(shifts), HEAD_DIM)
-        for shifts in SHIFTS
+        rows([own, came[0][0], came[1][0], came[0][1], came[1][1]]),
+        rows([came[2][0], mid, came[2][1]]),
     ]
     far, near_there = [], []
     for part in near:
@@ -294,20 +328,20 @@
     there = near_there + [lax.ppermute(part, "c", swap) for part in far]
     outs = {}
     shape = (BLOCK, GROUP * HEAD_DIM)
-    for mask in (4, 0):
+    for first, count in ((4, 4), (1, 3), (0, 1)):
         results = pl.pallas_call(
-            functools.partial(span_kernel, mask),
-            out_shape=[jax.ShapeDtypeStruct(shape, bf)] * 4,
+            functools.partial(span_kernel, first),
+            out_shape=[jax.ShapeDtypeStruct(shape, bf)] * count,
             in_specs=[SMEM] + [VMEM] * (1 + 4 * GROUPS),
-            out_specs=[VMEM] * 4,
-            scratch_shapes=KV_SCRATCH + [pltpu.VMEM((4,) + shape, bf)],
+            out_specs=[VMEM] * count,
+            scratch_shapes=KV_SCRATCH + [pltpu.VMEM((count,) + shape, bf)],
             compiler_params=room(24),
             cost_estimate=pl.CostEstimate(
                 flops=1 << 30, bytes_accessed=1 << 21, transcendentals=1 << 20
             ),
         )(slots, members, *here, *there)
         for n, out in enumerate(results):
-            step = mask ^ n
+            step = first + n
             pairs = [(m, m ^ step) for m in range(KV_HEADS)]
             outs[step] = lax.ppermute(out, HEAD_AXES, pairs) if step else out
     return [outs[step] for step in range(KV_HEADS)]
@@ -317,9 +351,12 @@
     return pl.pallas_call(
         join_kernel,
         out_shape=jax.ShapeDtypeStruct((BLOCK, HEADS * HEAD_DIM), jnp.bfloat16),
-        in_specs=[VMEM] * KV_HEADS,
+        in_specs=[HBM] * KV_HEADS,
         out_specs=HBM,
-        scratch_shapes=[pltpu.SemaphoreType.DMA((KV_HEADS,))],
+        scratch_shapes=[
+            pltpu.VMEM((KV_HEADS, BLOCK, GROUP * HEAD_DIM), jnp.bfloat16),
+            pltpu.SemaphoreType.DMA((2, KV_HEADS)),
+        ],
         compiler_params=pltpu.CompilerParams(vmem_limit_bytes=67043328),
     )(*outs)
 

time: 106 us -> 107 us (level)
  the two profiles are of different devices: /device:TPU:4 before, /device:TPU:1 now
where the time goes in v1:
time: 107 us
  starting transfers between devices  43.4 us (41%)
  waiting for transfers between devices  32.7 us (31%)
  Pallas kernels  24.5 us (23%)
  local copies, waits for them, and re-layouts  4.97 us (5%)
    all_to_all x1, starting transfers between devices, shards(): lax.all_to_all(send.reshape(DEVICES, 8, HEAD_DIM), AXES, 0, 0, tiled=True)  15.7 us
    pallas_call x3, Pallas kernels, quick(): pl.pallas_call(functools.partial(span_kernel, first), out_shape=[jax.Shap...  12.2 us
    ppermute x7, starting transfers between devices, quick(): outs[step] = lax.ppermute(out, HEAD_AXES, pairs) if step else out  9.95 us
    all_to_all x1, waiting for transfers between devices, shards(): lax.all_to_all(send.reshape(DEVICES, 8, HEAD_DIM), AXES, 0, 0, tiled=True)  9.89 us
    ppermute x2, waiting for transfers between devices, quick(): far.append(lax.ppermute(part, 'xh', swap))  8.63 us
    ppermute x7, waiting for transfers between devices, quick(): outs[step] = lax.ppermute(out, HEAD_AXES, pairs) if step else out  5.96 us
    ppermute x3, waiting for transfers between devices, quick(): came.append(lax.ppermute(jnp.stack([keep[j], taken[j]]), ('z', 'c'), pairs))  5.75 us
    ppermute x3, starting transfers between devices, quick(): came.append(lax.ppermute(jnp.stack([keep[j], taken[j]]), ('z', 'c'), pairs))  5.23 us
  transfers between devices with their start and end apart: 20, of which 7 were waited for; matrix products, arithmetic and copies ran while one was open for 0% of the time, Pallas kernels for 14%

profile of v1, /device:TPU:1, one launch (start us, length us, event | category | flops | bytes accessed | tf_op | source)
XLA Modules:
  0.0 106.5 jit_solution(8454029625372453306)
XLA Ops:
  0.0 2.8 %shard_map.76 = (bf16[8,2,4,2,2,8,128]{6,5,4,3,2,1,0:T(8,128)(2,1)}, f32[128,128]{1,0:T(8,128)}, f32[128,128]{1,0:T(8,128)}, bf16[128,1024]{1,0:T(8,128)(2,1)}) custom-call(s32[32768]{0:T(1024)} %pos_ref.1, f32[1,128]{1,0:T(1,128)} %constant.46.clone.inv_ref, bf16[128,1024]{1,0:T(8,128)(2,1)} %k_hbm.1, bf16[128,1024]{1,0:T(8,128)(2,1)} %v_ref.1), custom_call_target="tpu_custom_call" | custom-call | tf_op jit(solution)/shard_map/pallas_call | solution.py:395
  2.8 15.7 %all-to-all-start.1 = ((bf16[256,8,128]{2,1,0:T(8,128)(2,1)}), bf16[256,8,128]{2,1,0:T(8,128)(2,1)S(1)}, u32[]{:S(2)}, u32[]{:S(2)}) async-start(bf16[256,8,128]{2,1,0:T(8,128)(2,1)} %bitcast.46), calls=%async_computation.1 | async-start | bytes 1048576 | tf_op jit(solution)/shard_map/all_to_all | solution.py:410
  18.5 2.0 %shard_map.75 = (s32[34,8]{1,0:T(8,128)S(1)}, s32[8,8]{1,0:T(8,128)S(1)}, s32[1,1]{1,0:T(1,128)}) custom-call(s32[256,128]{1,0:T(8,128)} %bitcast.47, s32[8,256]{1,0:T(8,128)} %bitcast.50), custom_call_target="tpu_custom_call" | custom-call | flops 4194304 | bytes 4194304 | tf_op jit(solution)/shard_map/pallas_call | solution.py:413
  20.5 0.0 copy-start
  20.5 1.2 %copy-done = bf16[128,4096]{1,0:T(8,128)(2,1)S(1)} copy-done((bf16[128,4096]{1,0:T(8,128)(2,1)S(1)}, bf16[128,4096]{1,0:T(8,128)(2,1)}, u32[]{:S(2)}) %copy-start) | copy-done | bytes 1048600
  21.7 0.0 copy-start.1
  21.7 0.9 copy-done.1
  22.7 0.0 copy-start.2
  22.7 0.9 copy-done.2
  23.6 0.0 copy-start.3
  23.6 0.8 copy-done.3
  24.5 0.0 copy-start.4
  24.5 0.8 copy-done.4
  25.3 4.1 %shard_map.77 = bf16[8,128,768]{2,1,0:T(8,128)(2,1)} custom-call(s32[1,1]{1,0:T(1,128)} %get-tuple-element.62.count_ref, f32[128,128]{1,0:T(8,128)S(1)} %copy-done.3, f32[128,128]{1,0:T(8,128)S(1)} %copy-done.4, bf16[128,4096]{1,0:T(8,128)(2,1)S(1)} %copy-done, bf16[128,1024]{1,0:T(8,128)(2,1)S(1)} %copy-done.2, bf16[128,1024]{1,0:T(8,128)(2,1)S(1)} %copy-done.1), custom_call_target="tpu_custom_call" | custom-call | flops 4194304 | bytes 4194304 | tf_op jit(solution)/shard_map/pallas_call | solution.py:424
  29.4 9.9 %all-to-all-done.1.src_ref = bf16[256,8,128]{2,1,0:T(8,128)(2,1)S(1)} async-done(((bf16[256,8,128]{2,1,0:T(8,128)(2,1)}), bf16[256,8,128]{2,1,0:T(8,128)(2,1)S(1)}, u32[]{:S(2)}, u32[]{:S(2)}) %all-to-all-start.1) | async-done | bytes 524320 | tf_op jit(solution)/shard_map/all_to_all | solution.py:410
  39.3 0.0 copy-start.5
  39.3 3.6 %all-to-all-start.2 = ((bf16[8,128,768]{2,1,0:T(8,128)(2,1)}), bf16[8,128,768]{2,1,0:T(8,128)(2,1)S(1)}, u32[]{:S(2)}, u32[]{:S(2)}) async-start(bf16[8,128,768]{2,1,0:T(8,128)(2,1)} %shard_map.77), calls=%async_computation.2 | async-start | bytes 3145728 | tf_op jit(solution)/shard_map/all_to_all | solution.py:433
  42.9 1.3 %shard_map.78 = (bf16[34,8,128]{2,1,0:T(8,128)(2,1)S(1)}, bf16[34,8,128]{2,1,0:T(8,128)(2,1)S(1)}, bf16[3,34,8,128]{3,2,1,0:T(8,128)(2,1)S(1)}, bf16[3,34,8,128]{3,2,1,0:T(8,128)(2,1)S(1)}) custom-call(s32[34,8]{1,0:T(8,128)S(1)} %get-tuple-element.68.picks_ref, bf16[256,8,128]{2,1,0:T(8,128)(2,1)S(1)} %all-to-all-done.1.src_ref), custom_call_target="tpu_custom_call" | custom-call | tf_op jit(solution)/shard_map/pallas_call | solution.py:293
  44.1 0.4 collective-permute-start.4
  44.6 1.6 %collective-permute-start = (bf16[3,34,8,128]{3,2,1,0:T(8,128)(2,1)S(1)}, bf16[3,34,8,128]{3,2,1,0:T(8,128)(2,1)S(1)}, u32[]{:S(2)}, u32[]{:S(2)}) collective-permute-start(bf16[3,34,8,128]{3,2,1,0:T(8,128)(2,1)S(1)} %get-tuple-element.71), channel_id=1, source_target_pairs={{0,16},{16,0},{1,17},{17,1},{2,18},{18,2},{3,19},{19,3},{4,20},{20... | collective-permute-start | bytes 626696 | tf_op jit(solution)/shard_map/ppermute | solution.py:305
  46.2 1.1 %collective-permute-done = bf16[3,34,8,128]{3,2,1,0:T(8,128)(2,1)S(1)} collective-permute-done((bf16[3,34,8,128]{3,2,1,0:T(8,128)(2,1)S(1)}, bf16[3,34,8,128]{3,2,1,0:T(8,128)(2,1)S(1)}, u32[]{:S(2)}, u32[]{:S(2)}) %collective-permute-start) | collective-permute-done | bytes 208928 | tf_op jit(solution)/shard_map/ppermute | solution.py:305
  47.3 1.9 %collective-permute-start.1 = (bf16[2,34,8,128]{3,2,1,0:T(8,128)(2,1)S(1)}, bf16[2,34,8,128]{3,2,1,0:T(8,128)(2,1)S(1)}, u32[]{:S(2)}, u32[]{:S(2)}) collective-permute-start(bf16[2,34,8,128]{3,2,1,0:T(8,128)(2,1)S(1)} %pad_maximum_fusion.1), channel_id=1, source_target_pairs={{0,32},{16,240},{32,64},{48,16},{64,96},{80,48},{96,128},{112,80},... | collective-permute-start | bytes 417800 | tf_op jit(solution)/shard_map/ppermute | solution.py:314
  49.2 2.1 %collective-permute-start.2 = (bf16[2,34,8,128]{3,2,1,0:T(8,128)(2,1)S(1)}, bf16[2,34,8,128]{3,2,1,0:T(8,128)(2,1)S(1)}, u32[]{:S(2)}, u32[]{:S(2)}) collective-permute-start(bf16[2,34,8,128]{3,2,1,0:T(8,128)(2,1)S(1)} %pad_maximum_fusion.2), channel_id=1, source_target_pairs={{0,64},{16,208},{32,96},{48,240},{64,128},{80,16},{96,160},{112,48... | collective-permute-start | bytes 417800 | tf_op jit(solution)/shard_map/ppermute | solution.py:314
  51.3 1.3 %collective-permute-start.3 = (bf16[2,34,8,128]{3,2,1,0:T(8,128)(2,1)S(1)}, bf16[2,34,8,128]{3,2,1,0:T(8,128)(2,1)S(1)}, u32[]{:S(2)}, u32[]{:S(2)}) collective-permute-start(bf16[2,34,8,128]{3,2,1,0:T(8,128)(2,1)S(1)} %pad_maximum_fusion.3), channel_id=1, source_target_pairs={{0,96},{16,176},{32,128},{48,208},{64,160},{80,240},{96,192},{112,... | collective-permute-start | bytes 417800 | tf_op jit(solution)/shard_map/ppermute | solution.py:314
  52.6 0.0 collective-permute-done.1
  52.6 5.7 %collective-permute-done.2 = bf16[2,34,8,128]{3,2,1,0:T(8,128)(2,1)S(1)} collective-permute-done((bf16[2,34,8,128]{3,2,1,0:T(8,128)(2,1)S(1)}, bf16[2,34,8,128]{3,2,1,0:T(8,128)(2,1)S(1)}, u32[]{:S(2)}, u32[]{:S(2)}) %collective-permute-start.2) | collective-permute-done | bytes 139296 | tf_op jit(solution)/shard_map/ppermute | solution.py:314
  58.4 0.0 copy-done.5
  58.4 0.1 copy.27
  58.5 0.9 collective-permute-start.5
  59.3 0.0 collective-permute-done.3
  59.4 0.0 collective-permute-done.4
  59.4 3.5 %collective-permute-start.6 = (bf16[34,24,128]{2,1,0:T(8,128)(2,1)S(1)}, bf16[34,24,128]{2,1,0:T(8,128)(2,1)S(1)}, u32[]{:S(2)}, u32[]{:S(2)}) collective-permute-start(bf16[34,24,128]{2,1,0:T(8,128)(2,1)S(1)} %copy_bitcast_fusion.1.refs_1_), channel_id=1, source_target_pairs={{0,2},{2,0},{1,3},{3,1},{4,6},{6,4},{5,7},{7,5},{8,10},{10,8},{9,1... | collective-permute-start | bytes 626696 | tf_op jit(solution)/shard_map/ppermute | solution.py:325
  62.9 1.9 %collective-permute-start.7 = (bf16[34,40,128]{2,1,0:T(8,128)(2,1)S(1)}, bf16[34,40,128]{2,1,0:T(8,128)(2,1)S(1)}, u32[]{:S(2)}, u32[]{:S(2)}) collective-permute-start(bf16[34,40,128]{2,1,0:T(8,128)(2,1)S(1)} %bitcast.39), channel_id=1, source_target_pairs={{0,16},{16,0},{1,17},{17,1},{2,18},{18,2},{3,19},{19,3},{4,20},{20... | collective-permute-start | bytes 1044488 | tf_op jit(solution)/shard_map/ppermute | solution.py:326
  64.8 5.4 %collective-permute-done.5.refs_2_ = bf16[34,40,128]{2,1,0:T(8,128)(2,1)S(1)} collective-permute-done((bf16[34,40,128]{2,1,0:T(8,128)(2,1)S(1)}, bf16[34,40,128]{2,1,0:T(8,128)(2,1)S(1)}, u32[]{:S(2)}, u32[]{:S(2)}) %collective-permute-start.5) | collective-permute-done | bytes 348192 | tf_op jit(solution)/shard_map/ppermute | solution.py:325
  70.2 0.0 collective-permute-start.9
  70.2 0.5 collective-permute-start.8
  70.7 3.2 %collective-permute-done.6.refs_3_ = bf16[34,24,128]{2,1,0:T(8,128)(2,1)S(1)} collective-permute-done((bf16[34,24,128]{2,1,0:T(8,128)(2,1)S(1)}, bf16[34,24,128]{2,1,0:T(8,128)(2,1)S(1)}, u32[]{:S(2)}, u32[]{:S(2)}) %collective-permute-start.6) | collective-permute-done | bytes 208928 | tf_op jit(solution)/shard_map/ppermute | solution.py:325
  73.9 0.2 collective-permute-start.10
  74.1 0.0 all-to-all-done.2.x_ref
  74.1 0.0 collective-permute-done.8.refs_5_
  74.1 0.0 collective-permute-done.7.refs_4_
  74.2 1.4 %collective-permute-done.10.refs_7_ = bf16[34,24,128]{2,1,0:T(8,128)(2,1)} collective-permute-done((bf16[34,24,128]{2,1,0:T(8,128)(2,1)S(1)}, bf16[34,24,128]{2,1,0:T(8,128)(2,1)}, u32[]{:S(2)}, u32[]{:S(2)}) %collective-permute-start.10) | collective-permute-done | bytes 208928 | tf_op jit(solution)/shard_map/ppermute | solution.py:328
  75.5 0.0 collective-permute-done.9.refs_6_
  75.5 4.2 %shard_map.80 = (bf16[128,512]{1,0:T(8,128)(2,1)S(1)}, bf16[128,512]{1,0:T(8,128)(2,1)S(1)}, bf16[128,512]{1,0:T(8,128)(2,1)S(1)}) custom-call(s32[8,8]{1,0:T(8,128)S(1)} %get-tuple-element.67.slots_ref, bf16[8,128,768]{2,1,0:T(8,128)(2,1)S(1)} %all-to-all-done.2.x_ref, bf16[34,40,128]{2,1,0:T(8,128)(2,1)S(1)} %bitcast.40, ...), custom_call_target="tpu_custom_call" | custom-call | flops 1073741824 | bytes 2097152 | tf_op jit(solution)/shard_map/pallas_call | solution.py:332
  79.7 1.9 %collective-permute-start.11 = (bf16[128,512]{1,0:T(8,128)(2,1)S(1)}, bf16[128,512]{1,0:T(8,128)(2,1)}, u32[]{:S(2)}, u32[]{:S(2)}) collective-permute-start(bf16[128,512]{1,0:T(8,128)(2,1)S(1)} %get-tuple-element.73), channel_id=1, source_target_pairs={{0,1},{1,0},{4,5},{5,4},{8,9},{9,8},{12,13},{13,12},{2,3},{3,2},{6... | collective-permute-start | bytes 393224 | tf_op jit(solution)/shard_map/ppermute | solution.py:346
  81.6 1.2 %collective-permute-start.12 = (bf16[128,512]{1,0:T(8,128)(2,1)S(1)}, bf16[128,512]{1,0:T(8,128)(2,1)}, u32[]{:S(2)}, u32[]{:S(2)}) collective-permute-start(bf16[128,512]{1,0:T(8,128)(2,1)S(1)} %get-tuple-element.74), channel_id=1, source_target_pairs={{0,4},{1,5},{4,0},{5,1},{8,12},{9,13},{12,8},{13,9},{2,6},{3,7},{6... | collective-permute-start | bytes 393224 | tf_op jit(solution)/shard_map/ppermute | solution.py:346
  82.7 0.3 collective-permute-start.13
  83.1 5.2 %shard_map.81 = (bf16[128,512]{1,0:T(8,128)(2,1)S(1)}, bf16[128,512]{1,0:T(8,128)(2,1)S(1)}, bf16[128,512]{1,0:T(8,128)(2,1)S(1)}, bf16[128,512]{1,0:T(8,128)(2,1)S(1)}) custom-call(s32[8,8]{1,0:T(8,128)S(1)} %get-tuple-element.67.slots_ref, bf16[8,128,768]{2,1,0:T(8,128)(2,1)S(1)} %all-to-all-done.2.x_ref, bf16[34,40,128]{2,1,0:T(8,128)(2,1)S(1)} %bitcast.41, ...), custom_call_target="tpu_custom_call" | custom-call | flops 1073741824 | bytes 2097152 | tf_op jit(solution)/shard_map/pallas_call | solution.py:332
  88.3 2.7 %collective-permute-start.14 = (bf16[128,512]{1,0:T(8,128)(2,1)S(1)}, bf16[128,512]{1,0:T(8,128)(2,1)}, u32[]{:S(2)}, u32[]{:S(2)}) collective-permute-start(bf16[128,512]{1,0:T(8,128)(2,1)S(1)} %get-tuple-element.76), channel_id=1, source_target_pairs={{0,8},{1,9},{4,12},{5,13},{8,0},{9,1},{12,4},{13,5},{2,10},{3,11},... | collective-permute-start | bytes 393224 | tf_op jit(solution)/shard_map/ppermute | solution.py:346
  91.0 1.2 %collective-permute-start.15 = (bf16[128,512]{1,0:T(8,128)(2,1)S(1)}, bf16[128,512]{1,0:T(8,128)(2,1)}, u32[]{:S(2)}, u32[]{:S(2)}) collective-permute-start(bf16[128,512]{1,0:T(8,128)(2,1)S(1)} %get-tuple-element.77), channel_id=1, source_target_pairs={{0,9},{1,8},{4,13},{5,12},{8,1},{9,0},{12,5},{13,4},{2,11},{3,10},... | collective-permute-start | bytes 393224 | tf_op jit(solution)/shard_map/ppermute | solution.py:346
  92.2 0.0 collective-permute-done.11
  92.3 2.3 %collective-permute-start.16 = (bf16[128,512]{1,0:T(8,128)(2,1)S(1)}, bf16[128,512]{1,0:T(8,128)(2,1)}, u32[]{:S(2)}, u32[]{:S(2)}) collective-permute-start(bf16[128,512]{1,0:T(8,128)(2,1)S(1)} %get-tuple-element.78), channel_id=1, source_target_pairs={{0,12},{1,13},{4,8},{5,9},{8,4},{9,5},{12,0},{13,1},{2,14},{3,15},... | collective-permute-start | bytes 393224 | tf_op jit(solution)/shard_map/ppermute | solution.py:346
  94.5 0.0 collective-permute-done.12
  94.5 0.4 collective-permute-start.17
  95.5 2.8 %shard_map.79 = bf16[128,512]{1,0:T(8,128)(2,1)} custom-call(s32[8,8]{1,0:T(8,128)S(1)} %get-tuple-element.67.slots_ref, bf16[8,128,768]{2,1,0:T(8,128)(2,1)S(1)} %all-to-all-done.2.x_ref, bf16[34,40,128]{2,1,0:T(8,128)(2,1)S(1)} %bitcast.42, bf16[34,24,128]{2,1,0:T(8,128)(2,1)S(1)} %copy_bitcast_fusion.1.refs_1_, ...), custom_call_target="tpu_custom_call" | custom-call | flops 1073741824 | bytes 2097152 | tf_op jit(solution)/shard_map/pallas_call | solution.py:332
  98.3 0.0 collective-permute-done.13
  98.3 0.0 collective-permute-done.14
  98.3 0.0 collective-permute-done.15
  98.3 5.9 %collective-permute-done.16 = bf16[128,512]{1,0:T(8,128)(2,1)} collective-permute-done((bf16[128,512]{1,0:T(8,128)(2,1)S(1)}, bf16[128,512]{1,0:T(8,128)(2,1)}, u32[]{:S(2)}, u32[]{:S(2)}) %collective-permute-start.16) | collective-permute-done | bytes 131104 | tf_op jit(solution)/shard_map/ppermute | solution.py:346
  104.2 0.0 collective-permute-done.17
  104.2 0.0 copy-done.7
  104.2 0.0 copy-done.8
  104.2 2.1 %conditional.1 = (bf16[128,4096]{1,0:T(8,128)(2,1)}) conditional(s32[]{:T(128)} %bitcast.8, (s32[32768]{0:T(1024)S(1)}, s32[256,8]{0,1:T(8,128)S(1)}, bf16[256,8,128]{2,1,0:T(8,128)(2,1)}, bf16[8,128,768]{2,1,0:T(8,128)(2,1)}) %tuple.30, (bf16[128,512]{1,0:T(8,128)(2,1)}, bf16[128,512]{1,0:T(8,128)(2,1)}, bf16[128,512]{1,0:T(8,128)(2,1)}, ...), branch_computations={%region_0.3_spmd, %region_3.4_spmd} | conditional | flops 208409 | bytes 20584806 | solution.py:436
  104.3 2.1 %branch_1_fun.1 = bf16[128,4096]{1,0:T(8,128)(2,1)} custom-call(bf16[128,512]{1,0:T(8,128)(2,1)} %get-tuple-element.36.refs_0_, bf16[128,512]{1,0:T(8,128)(2,1)} %get-tuple-element.37.refs_1_, bf16[128,512]{1,0:T(8,128)(2,1)} %get-tuple-element.38.refs_2_, bf16[128,512]{1,0:T(8,128)(2,1)} %get-tuple-element.39.refs_3_, ...), custom_call_target="tpu_custom_call" | custom-call | tf_op jit(solution)/shard_map/cond/branch_1_fun/pallas_call | solution.py:351
  (14 shorter events, 0.2 us)
Async XLA Ops:
  2.8 36.5 %all-to-all-start.1 = ((bf16[256,8,128]{2,1,0:T(8,128)(2,1)}), bf16[256,8,128]{2,1,0:T(8,128)(2,1)S(1)}, u32[]{:S(2)}, u32[]{:S(2)}) async-start(bf16[256,8,128]{2,1,0:T(8,128)(2,1)} %bitcast.46), calls=%async_computation.1 | async-start | bytes 1048576 | tf_op jit(solution)/shard_map/all_to_all | solution.py:410
  20.5 1.2 %copy-start = (bf16[128,4096]{1,0:T(8,128)(2,1)S(1)}, bf16[128,4096]{1,0:T(8,128)(2,1)}, u32[]{:S(2)}) copy-start(bf16[128,4096]{1,0:T(8,128)(2,1)} %q_ref.1) | copy-start | bytes 3145732
  21.7 0.9 copy-start.1
  22.7 0.9 copy-start.2
  23.6 0.8 copy-start.3
  24.5 0.8 copy-start.4
  39.3 19.1 %copy-start.5 = (bf16[256,8,128]{2,1,0:T(8,128)(2,1)}, bf16[256,8,128]{2,1,0:T(8,128)(2,1)S(1)}, u32[]{:S(2)}) copy-start(bf16[256,8,128]{2,1,0:T(8,128)(2,1)S(1)} %all-to-all-done.1.src_ref) | copy-start | bytes 1572868
  39.3 34.9 %all-to-all-start.2 = ((bf16[8,128,768]{2,1,0:T(8,128)(2,1)}), bf16[8,128,768]{2,1,0:T(8,128)(2,1)S(1)}, u32[]{:S(2)}, u32[]{:S(2)}) async-start(bf16[8,128,768]{2,1,0:T(8,128)(2,1)} %shard_map.77), calls=%async_computation.2 | async-start | bytes 3145728 | tf_op jit(solution)/shard_map/all_to_all | solution.py:433
  44.1 15.2 %collective-permute-start.4 = (bf16[34,8,128]{2,1,0:T(8,128)(2,1)S(1)}, bf16[34,8,128]{2,1,0:T(8,128)(2,1)S(1)}, u32[]{:S(2)}, u32[]{:S(2)}) collective-permute-start(bf16[34,8,128]{2,1,0:T(8,128)(2,1)S(1)} %get-tuple-element.72), channel_id=1, source_target_pairs={{0,128},{32,160},{64,192},{96,224},{128,0},{160,32},{192,64},{224,... | collective-permute-start | bytes 208904 | tf_op jit(solution)/shard_map/ppermute | solution.py:306
  44.6 2.7 %collective-permute-start = (bf16[3,34,8,128]{3,2,1,0:T(8,128)(2,1)S(1)}, bf16[3,34,8,128]{3,2,1,0:T(8,128)(2,1)S(1)}, u32[]{:S(2)}, u32[]{:S(2)}) collective-permute-start(bf16[3,34,8,128]{3,2,1,0:T(8,128)(2,1)S(1)} %get-tuple-element.71), channel_id=1, source_target_pairs={{0,16},{16,0},{1,17},{17,1},{2,18},{18,2},{3,19},{19,3},{4,20},{20... | collective-permute-start | bytes 626696 | tf_op jit(solution)/shard_map/ppermute | solution.py:305
  47.3 5.3 %collective-permute-start.1 = (bf16[2,34,8,128]{3,2,1,0:T(8,128)(2,1)S(1)}, bf16[2,34,8,128]{3,2,1,0:T(8,128)(2,1)S(1)}, u32[]{:S(2)}, u32[]{:S(2)}) collective-permute-start(bf16[2,34,8,128]{3,2,1,0:T(8,128)(2,1)S(1)} %pad_maximum_fusion.1), channel_id=1, source_target_pairs={{0,32},{16,240},{32,64},{48,16},{64,96},{80,48},{96,128},{112,80},... | collective-permute-start | bytes 417800 | tf_op jit(solution)/shard_map/ppermute | solution.py:314
  49.2 9.1 %collective-permute-start.2 = (bf16[2,34,8,128]{3,2,1,0:T(8,128)(2,1)S(1)}, bf16[2,34,8,128]{3,2,1,0:T(8,128)(2,1)S(1)}, u32[]{:S(2)}, u32[]{:S(2)}) collective-permute-start(bf16[2,34,8,128]{3,2,1,0:T(8,128)(2,1)S(1)} %pad_maximum_fusion.2), channel_id=1, source_target_pairs={{0,64},{16,208},{32,96},{48,240},{64,128},{80,16},{96,160},{112,48... | collective-permute-start | bytes 417800 | tf_op jit(solution)/shard_map/ppermute | solution.py:314
  51.3 8.0 %collective-permute-start.3 = (bf16[2,34,8,128]{3,2,1,0:T(8,128)(2,1)S(1)}, bf16[2,34,8,128]{3,2,1,0:T(8,128)(2,1)S(1)}, u32[]{:S(2)}, u32[]{:S(2)}) collective-permute-start(bf16[2,34,8,128]{3,2,1,0:T(8,128)(2,1)S(1)} %pad_maximum_fusion.3), channel_id=1, source_target_pairs={{0,96},{16,176},{32,128},{48,208},{64,160},{80,240},{96,192},{112,... | collective-permute-start | bytes 417800 | tf_op jit(solution)/shard_map/ppermute | solution.py:314
  58.5 11.8 %collective-permute-start.5 = (bf16[34,40,128]{2,1,0:T(8,128)(2,1)S(1)}, bf16[34,40,128]{2,1,0:T(8,128)(2,1)S(1)}, u32[]{:S(2)}, u32[]{:S(2)}) collective-permute-start(bf16[34,40,128]{2,1,0:T(8,128)(2,1)S(1)} %bitcast.38), channel_id=1, source_target_pairs={{0,2},{2,0},{1,3},{3,1},{4,6},{6,4},{5,7},{7,5},{8,10},{10,8},{9,1... | collective-permute-start | bytes 1044488 | tf_op jit(solution)/shard_map/ppermute | solution.py:325
  59.4 14.5 %collective-permute-start.6 = (bf16[34,24,128]{2,1,0:T(8,128)(2,1)S(1)}, bf16[34,24,128]{2,1,0:T(8,128)(2,1)S(1)}, u32[]{:S(2)}, u32[]{:S(2)}) collective-permute-start(bf16[34,24,128]{2,1,0:T(8,128)(2,1)S(1)} %copy_bitcast_fusion.1.refs_1_), channel_id=1, source_target_pairs={{0,2},{2,0},{1,3},{3,1},{4,6},{6,4},{5,7},{7,5},{8,10},{10,8},{9,1... | collective-permute-start | bytes 626696 | tf_op jit(solution)/shard_map/ppermute | solution.py:325
  62.9 11.3 %collective-permute-start.7 = (bf16[34,40,128]{2,1,0:T(8,128)(2,1)S(1)}, bf16[34,40,128]{2,1,0:T(8,128)(2,1)S(1)}, u32[]{:S(2)}, u32[]{:S(2)}) collective-permute-start(bf16[34,40,128]{2,1,0:T(8,128)(2,1)S(1)} %bitcast.39), channel_id=1, source_target_pairs={{0,16},{16,0},{1,17},{17,1},{2,18},{18,2},{3,19},{19,3},{4,20},{20... | collective-permute-start | bytes 1044488 | tf_op jit(solution)/shard_map/ppermute | solution.py:326
  70.2 5.3 %collective-permute-start.9 = (bf16[34,40,128]{2,1,0:T(8,128)(2,1)S(1)}, bf16[34,40,128]{2,1,0:T(8,128)(2,1)S(1)}, u32[]{:S(2)}, u32[]{:S(2)}) collective-permute-start(bf16[34,40,128]{2,1,0:T(8,128)(2,1)S(1)} %collective-permute-done.5.refs_2_), channel_id=1, source_target_pairs={{0,16},{16,0},{1,17},{17,1},{2,18},{18,2},{3,19},{19,3},{4,20},{20... | collective-permute-start | bytes 1044488 | tf_op jit(solution)/shard_map/ppermute | solution.py:328
  70.2 3.9 %collective-permute-start.8 = (bf16[34,24,128]{2,1,0:T(8,128)(2,1)S(1)}, bf16[34,24,128]{2,1,0:T(8,128)(2,1)}, u32[]{:S(2)}, u32[]{:S(2)}) collective-permute-start(bf16[34,24,128]{2,1,0:T(8,128)(2,1)S(1)} %copy_bitcast_fusion.1.refs_1_), channel_id=1, source_target_pairs={{0,16},{16,0},{1,17},{17,1},{2,18},{18,2},{3,19},{19,3},{4,20},{20... | collective-permute-start | bytes 626696 | tf_op jit(solution)/shard_map/ppermute | solution.py:326
  73.9 1.6 %collective-permute-start.10 = (bf16[34,24,128]{2,1,0:T(8,128)(2,1)S(1)}, bf16[34,24,128]{2,1,0:T(8,128)(2,1)}, u32[]{:S(2)}, u32[]{:S(2)}) collective-permute-start(bf16[34,24,128]{2,1,0:T(8,128)(2,1)S(1)} %collective-permute-done.6.refs_3_), channel_id=1, source_target_pairs={{0,16},{16,0},{1,17},{17,1},{2,18},{18,2},{3,19},{19,3},{4,20},{20... | collective-permute-start | bytes 626696 | tf_op jit(solution)/shard_map/ppermute | solution.py:328
  79.7 12.5 %collective-permute-start.11 = (bf16[128,512]{1,0:T(8,128)(2,1)S(1)}, bf16[128,512]{1,0:T(8,128)(2,1)}, u32[]{:S(2)}, u32[]{:S(2)}) collective-permute-start(bf16[128,512]{1,0:T(8,128)(2,1)S(1)} %get-tuple-element.73), channel_id=1, source_target_pairs={{0,1},{1,0},{4,5},{5,4},{8,9},{9,8},{12,13},{13,12},{2,3},{3,2},{6... | collective-permute-start | bytes 393224 | tf_op jit(solution)/shard_map/ppermute | solution.py:346
  81.6 13.0 %collective-permute-start.12 = (bf16[128,512]{1,0:T(8,128)(2,1)S(1)}, bf16[128,512]{1,0:T(8,128)(2,1)}, u32[]{:S(2)}, u32[]{:S(2)}) collective-permute-start(bf16[128,512]{1,0:T(8,128)(2,1)S(1)} %get-tuple-element.74), channel_id=1, source_target_pairs={{0,4},{1,5},{4,0},{5,1},{8,12},{9,13},{12,8},{13,9},{2,6},{3,7},{6... | collective-permute-start | bytes 393224 | tf_op jit(solution)/shard_map/ppermute | solution.py:346
  82.7 21.5 %copy-start.7 = (s32[32768]{0:T(1024)S(1)}, s32[32768]{0:T(1024)}, u32[]{:S(2)}) copy-start(s32[32768]{0:T(1024)} %param.13) | copy-start | bytes 393220
  82.7 21.5 %copy-start.8 = (s32[256,8]{0,1:T(8,128)S(1)}, s32[256,8]{0,1:T(8,128)}, u32[]{:S(2)}) copy-start(s32[256,8]{0,1:T(8,128)} %param.12) | copy-start | bytes 24580
  82.7 15.5 %collective-permute-start.13 = (bf16[128,512]{1,0:T(8,128)(2,1)S(1)}, bf16[128,512]{1,0:T(8,128)(2,1)}, u32[]{:S(2)}, u32[]{:S(2)}) collective-permute-start(bf16[128,512]{1,0:T(8,128)(2,1)S(1)} %get-tuple-element.75), channel_id=1, source_target_pairs={{0,5},{1,4},{4,1},{5,0},{8,13},{9,12},{12,9},{13,8},{2,7},{3,6},{6... | collective-permute-start | bytes 393224 | tf_op jit(solution)/shard_map/ppermute | solution.py:346
  88.3 10.0 %collective-permute-start.14 = (bf16[128,512]{1,0:T(8,128)(2,1)S(1)}, bf16[128,512]{1,0:T(8,128)(2,1)}, u32[]{:S(2)}, u32[]{:S(2)}) collective-permute-start(bf16[128,512]{1,0:T(8,128)(2,1)S(1)} %get-tuple-element.76), channel_id=1, source_target_pairs={{0,8},{1,9},{4,12},{5,13},{8,0},{9,1},{12,4},{13,5},{2,10},{3,11},... | collective-permute-start | bytes 393224 | tf_op jit(solution)/shard_map/ppermute | solution.py:346
  91.0 7.3 %collective-permute-start.15 = (bf16[128,512]{1,0:T(8,128)(2,1)S(1)}, bf16[128,512]{1,0:T(8,128)(2,1)}, u32[]{:S(2)}, u32[]{:S(2)}) collective-permute-start(bf16[128,512]{1,0:T(8,128)(2,1)S(1)} %get-tuple-element.77), channel_id=1, source_target_pairs={{0,9},{1,8},{4,13},{5,12},{8,1},{9,0},{12,5},{13,4},{2,11},{3,10},... | collective-permute-start | bytes 393224 | tf_op jit(solution)/shard_map/ppermute | solution.py:346
  92.3 12.0 %collective-permute-start.16 = (bf16[128,512]{1,0:T(8,128)(2,1)S(1)}, bf16[128,512]{1,0:T(8,128)(2,1)}, u32[]{:S(2)}, u32[]{:S(2)}) collective-permute-start(bf16[128,512]{1,0:T(8,128)(2,1)S(1)} %get-tuple-element.78), channel_id=1, source_target_pairs={{0,12},{1,13},{4,8},{5,9},{8,4},{9,5},{12,0},{13,1},{2,14},{3,15},... | collective-permute-start | bytes 393224 | tf_op jit(solution)/shard_map/ppermute | solution.py:346
  94.5 9.7 %collective-permute-start.17 = (bf16[128,512]{1,0:T(8,128)(2,1)S(1)}, bf16[128,512]{1,0:T(8,128)(2,1)}, u32[]{:S(2)}, u32[]{:S(2)}) collective-permute-start(bf16[128,512]{1,0:T(8,128)(2,1)S(1)} %get-tuple-element.79), channel_id=1, source_target_pairs={{0,13},{1,12},{4,9},{5,8},{8,5},{9,4},{12,1},{13,0},{2,15},{3,14},... | collective-permute-start | bytes 393224 | tf_op jit(solution)/shard_map/ppermute | solution.py:346

commit v2 on v1

--- a/solution.py
+++ b/solution.py
@@ -37,7 +37,6 @@
 HBM = pl.BlockSpec(memory_space=pltpu.HBM)
 SMEM = pl.BlockSpec(memory_space=pltpu.SMEM)
 VMEM = pl.BlockSpec(memory_space=pltpu.VMEM)
-VMEM_ONE = pl.BlockSpec((1, 1), lambda h: (0, 0))
 
 
 def room(mib):
@@ -90,11 +89,12 @@
         for high in range(2):
             for low in range(8):
                 t = (high * 8 + low) * 8
-                send_ref[low, 0, h // 2, high, h % 2] = turned[t : t + 8]
-                send_ref[low, 1, h // 2, high, h % 2] = plain[t : t + 8]
-
-
-def bundle_kernel(count_ref, cos_ref, sin_ref, q_ref, k_ref, v_ref, out_ref):
+                xl = h % 2 ^ high
+                send_ref[low, 0, h // 2, high, xl] = turned[t : t + 8]
+                send_ref[low, 1, h // 2, high, xl] = plain[t : t + 8]
+
+
+def bundle_kernel(xh_ref, count_ref, cos_ref, sin_ref, q_ref, k_ref, v_ref, out_ref):
     for g in range(GROUP):
         cols = slice(g * HEAD_DIM, (g + 1) * HEAD_DIM)
         out_ref[:, cols] = turn(q_ref[:, cols], cos_ref[...], sin_ref[...])
@@ -274,7 +274,7 @@
     width = GROUP * HEAD_DIM
     loads, stores = [], []
     for step in range(KV_HEADS):
-        at = pl.multiple_of((own_member() ^ step) * width, width)
+        at = pl.multiple_of((own_member() ^ step ^ lax.axis_index("xh")) * width, width)
         held = held_ref.at[step]
         loads.append(pltpu.make_async_copy(refs[step], held, sems.at[0, step]))
         stores.append(pltpu.make_async_copy(held, out_ref.at[:, pl.ds(at, width)], sems.at[1, step]))
@@ -322,8 +322,9 @@
     ]
     far, near_there = [], []
     for part in near:
-        far.append(lax.ppermute(part, "xh", swap))
+        far.append(lax.ppermute(part, ("xh", "xl"), [(x, 3 - x) for x in range(4)]))
         near_there.append(lax.ppermute(part, "c", swap))
+    far[1], members = lax.optimization_barrier((far[1], members))
     here = near + far
     there = near_there + [lax.ppermute(part, "c", swap) for part in far]
     outs = {}
@@ -376,8 +377,13 @@
         in_specs=[SMEM, VMEM],
     )(spans, chunks)
     got = lax.all_to_all(packed.reshape(DEVICES, SLOTS * 8, HEAD_DIM), AXES, 0, 0, tiled=True)
-    got = got.reshape(8, 2, 4, 2, 2, SLOTS, 8, HEAD_DIM).transpose(1, 2, 4, 3, 5, 0, 6, 7)
+    got = got.reshape(8, 2, 4, 2, 2, SLOTS, 8, HEAD_DIM)
+    got = jnp.stack([got[:, :, :, 0], got[:, :, :, 1, ::-1]], axis=3)
+    got = got.transpose(1, 2, 4, 3, 5, 0, 6, 7)
     got = got.reshape(2, KV_HEADS, SLOTS * BLOCK, HEAD_DIM)
+    pairs = bundle.reshape(KV_HEADS // 2, 2, BLOCK, PACK)
+    pairs = jnp.where(lax.axis_index("xh") == 0, pairs, pairs[:, ::-1])
+    bundle = pairs.reshape(bundle.shape)
     far_k = pl.BlockSpec((None, None, SLOTS * BLOCK, HEAD_DIM), lambda h: (0, h, 0, 0))
     far_v = pl.BlockSpec((None, None, SLOTS * BLOCK, HEAD_DIM), lambda h: (1, h, 0, 0))
     return pl.pallas_call(
@@ -408,8 +414,10 @@
         ],
     )(positions, jnp.asarray(inverse_row()), keys, values)
     chunks = lax.all_to_all(send.reshape(DEVICES, 8, HEAD_DIM), AXES, 0, 0, tiled=True)
-    table = pl.BlockSpec((BLOCK, HEAD_DIM), lambda h: (0, 0))
-    head = pl.BlockSpec((BLOCK, HEAD_DIM), lambda h: (0, h))
+    table = pl.BlockSpec((BLOCK, HEAD_DIM), lambda h, xh: (0, 0))
+    head = pl.BlockSpec((BLOCK, HEAD_DIM), lambda h, xh: (0, h))
+    one = pl.BlockSpec((1, 1), lambda h, xh: (0, 0))
+    heads = pl.BlockSpec((BLOCK, GROUP * HEAD_DIM), lambda h, xh: (0, h))
     picks, slots, count = pl.pallas_call(
         plan_kernel,
         out_shape=(
@@ -423,13 +431,16 @@
     )(token_block.reshape(DEVICES, BLOCK), ancestors.T)
     bundle = pl.pallas_call(
         bundle_kernel,
-        grid=(KV_HEADS,),
+        grid_spec=pltpu.PrefetchScalarGridSpec(
+            num_scalar_prefetch=1,
+            grid=(KV_HEADS,),
+            in_specs=[one, table, table, heads, head, head],
+            out_specs=pl.BlockSpec((None, BLOCK, PACK), lambda h, xh: (h ^ xh[0], 0, 0)),
+        ),
         out_shape=jax.ShapeDtypeStruct((KV_HEADS, BLOCK, PACK), bf),
-        in_specs=[VMEM_ONE, table, table, pl.BlockSpec((BLOCK, GROUP * HEAD_DIM), lambda h: (0, h)), head, head],
-        out_specs=pl.BlockSpec((None, BLOCK, PACK), lambda h: (h, 0, 0)),
         compiler_params=room(8),
         cost_estimate=pl.CostEstimate(flops=4 << 20, bytes_accessed=4 << 20, transcendentals=0),
-    )(count, cosine, sine, queries, own_k, values)
+    )(lax.axis_index("xh").astype(i32)[None], count, cosine, sine, queries, own_k, values)
     members = lax.all_to_all(bundle, HEAD_AXES, 0, 0, tiled=True)
     fits = count[0, 0] <= CAP
     outs = quick(picks, slots, chunks, members)

time: 107 us -> 101 us (0.944); the launches traced: 107 us -> 99.2 us
  waiting for transfers between devices: 32.7 us -> 27 us
  local copies, waits for them, and re-layouts: 4.97 us -> 2.81 us
    ppermute x7, waiting for transfers between devices: 5.96 us -> 0.33 us  [quick(): outs[step] = lax.ppermute(out, HEAD_AXES, pairs) if step else out]
    ppermute x2, starting transfers between devices: 2.42 us -> 5.35 us  [quick(): near_there.append(lax.ppermute(part, 'c', swap))]
    unnamed x20, local copies, waits for them, and re-layouts: 4.86 us -> 2.7 us
    all_to_all x1, waiting for transfers between devices: 9.89 us -> 11.9 us  [shards(): lax.all_to_all(send.reshape(DEVICES, 8, HEAD_DIM), AXES, 0, 0, tiled=True)]
    ppermute x2, waiting for transfers between devices: 8.63 us -> 6.64 us  [quick(): far.append(lax.ppermute(part, ('xh', 'xl'), [(x, 3 - x) for x in range(4)]))]
    ppermute x2, starting transfers between devices: 4.34 us -> 2.85 us  [quick(): far.append(lax.ppermute(part, ('xh', 'xl'), [(x, 3 - x) for x in range(4)]))]
    ppermute x1, starting transfers between devices: 1.63 us -> 0.18 us  [quick(): taken = lax.ppermute(give, 'c', swap)]
    ppermute x1, starting transfers between devices: 0.4 us -> 1.57 us  [quick(): mid = lax.ppermute(mid, 'z', [(i, (i + 4) % PLANES) for i in range(PLANES)])]
where the time goes in v2:
time: 101 us; the launch traced here: 99.2 us
  starting transfers between devices  43.9 us (43%)
  waiting for transfers between devices  27 us (27%)
  Pallas kernels  24.4 us (24%)
  local copies, waits for them, and re-layouts  2.81 us (3%)
    all_to_all x1, starting transfers between devices, shards(): lax.all_to_all(send.reshape(DEVICES, 8, HEAD_DIM), AXES, 0, 0, tiled=True)  15.7 us
    all_to_all x1, waiting for transfers between devices, shards(): lax.all_to_all(send.reshape(DEVICES, 8, HEAD_DIM), AXES, 0, 0, tiled=True)  11.9 us
    pallas_call x3, Pallas kernels, quick(): pl.pallas_call(functools.partial(span_kernel, first), out_shape=[jax.Shap...  11.9 us
    ppermute x7, starting transfers between devices, quick(): outs[step] = lax.ppermute(out, HEAD_AXES, pairs) if step else out  9.5 us
    ppermute x2, waiting for transfers between devices, quick(): far.append(lax.ppermute(part, ('xh', 'xl'), [(x, 3 - x) for x in range(4)]))  6.64 us
    ppermute x3, waiting for transfers between devices, quick(): came.append(lax.ppermute(jnp.stack([keep[j], taken[j]]), ('z', 'c'), pairs))  6.63 us
    ppermute x2, starting transfers between devices, quick(): near_there.append(lax.ppermute(part, 'c', swap))  5.35 us
    ppermute x3, starting transfers between devices, quick(): came.append(lax.ppermute(jnp.stack([keep[j], taken[j]]), ('z', 'c'), pairs))  5.23 us
  transfers between devices with their start and end apart: 20, of which 7 were waited for; matrix products, arithmetic and copies ran while one was open for 0% of the time, Pallas kernels for 14%

profile of v2, /device:TPU:1, one launch (start us, length us, event | category | flops | bytes accessed | tf_op | source)
XLA Modules:
  0.0 99.2 jit_solution(5747583767998398649)
XLA Ops:
  0.0 0.0 copy-start
  0.0 0.0 copy-start.1
  0.0 2.9 %shard_map.76 = (bf16[8,2,4,2,2,8,128]{6,5,4,3,2,1,0:T(8,128)(2,1)}, f32[128,128]{1,0:T(8,128)}, f32[128,128]{1,0:T(8,128)}, bf16[128,1024]{1,0:T(8,128)(2,1)}) custom-call(s32[32768]{0:T(1024)} %pos_ref.1, f32[1,128]{1,0:T(1,128)} %constant.50.clone.inv_ref, bf16[128,1024]{1,0:T(8,128)(2,1)} %k_hbm.1, bf16[128,1024]{1,0:T(8,128)(2,1)} %v_ref.1), custom_call_target="tpu_custom_call" | custom-call | tf_op jit(solution)/shard_map/pallas_call | solution.py:401
  2.9 15.7 %all-to-all-start.1 = ((bf16[256,8,128]{2,1,0:T(8,128)(2,1)}), bf16[256,8,128]{2,1,0:T(8,128)(2,1)S(1)}, u32[]{:S(2)}, u32[]{:S(2)}) async-start(bf16[256,8,128]{2,1,0:T(8,128)(2,1)} %bitcast.50), calls=%async_computation.1 | async-start | bytes 1048576 | tf_op jit(solution)/shard_map/all_to_all | solution.py:416
  18.6 2.1 %shard_map.75 = (s32[34,8]{1,0:T(8,128)S(1)}, s32[8,8]{1,0:T(8,128)S(1)}, s32[1,1]{1,0:T(1,128)}) custom-call(s32[256,128]{1,0:T(8,128)} %bitcast.51, s32[8,256]{1,0:T(8,128)} %bitcast.54), custom_call_target="tpu_custom_call" | custom-call | flops 4194304 | bytes 4194304 | tf_op jit(solution)/shard_map/pallas_call | solution.py:421
  20.7 0.0 copy-done
  20.7 0.0 copy-done.1
  20.7 0.0 copy-start.2
  20.7 0.9 copy-done.2
  21.6 0.0 copy-start.3
  21.6 0.8 copy-done.3
  22.5 0.8 copy-done.4
  23.3 4.2 %shard_map.77 = bf16[8,128,768]{2,1,0:T(8,128)(2,1)} custom-call(s32[1]{0:T(128)} %bitcast.10.xh_ref, s32[1,1]{1,0:T(1,128)} %get-tuple-element.64.count_ref, f32[128,128]{1,0:T(8,128)S(1)} %copy-done.3, f32[128,128]{1,0:T(8,128)S(1)} %copy-done.4, bf16[128,4096]{1,0:T(8,128)(2,1)S(1)} %copy-done.1, bf16[128,1024]{1,0:T(8,128)(2,1)S(1)} %copy-done.2, ...), custom_call_target="tpu_custom_call" | custom-call | flops 4194304 | bytes 4194304 | tf_op jit(solution)/shard_map/pallas_call | solution.py:432
  27.5 11.9 %all-to-all-done.1.src_ref = bf16[256,8,128]{2,1,0:T(8,128)(2,1)S(1)} async-done(((bf16[256,8,128]{2,1,0:T(8,128)(2,1)}), bf16[256,8,128]{2,1,0:T(8,128)(2,1)S(1)}, u32[]{:S(2)}, u32[]{:S(2)}) %all-to-all-start.1) | async-done | bytes 524320 | tf_op jit(solution)/shard_map/all_to_all | solution.py:416
  39.4 3.6 %all-to-all-start.2 = ((bf16[8,128,768]{2,1,0:T(8,128)(2,1)}), bf16[8,128,768]{2,1,0:T(8,128)(2,1)S(1)}, u32[]{:S(2)}, u32[]{:S(2)}) async-start(bf16[8,128,768]{2,1,0:T(8,128)(2,1)} %shard_map.77), calls=%async_computation.2 | async-start | bytes 3145728 | tf_op jit(solution)/shard_map/all_to_all | solution.py:444
  43.0 1.3 %shard_map.78 = (bf16[34,8,128]{2,1,0:T(8,128)(2,1)S(1)}, bf16[34,8,128]{2,1,0:T(8,128)(2,1)S(1)}, bf16[3,34,8,128]{3,2,1,0:T(8,128)(2,1)S(1)}, bf16[3,34,8,128]{3,2,1,0:T(8,128)(2,1)S(1)}) custom-call(s32[34,8]{1,0:T(8,128)S(1)} %get-tuple-element.70.picks_ref, bf16[256,8,128]{2,1,0:T(8,128)(2,1)S(1)} %all-to-all-done.1.src_ref), custom_call_target="tpu_custom_call" | custom-call | tf_op jit(solution)/shard_map/pallas_call | solution.py:293
  44.2 0.0 copy-done.5
  44.3 0.2 collective-permute-start
  44.5 1.6 %collective-permute-start.2 = (bf16[34,8,128]{2,1,0:T(8,128)(2,1)S(1)}, bf16[34,8,128]{2,1,0:T(8,128)(2,1)S(1)}, u32[]{:S(2)}, u32[]{:S(2)}) collective-permute-start(bf16[34,8,128]{2,1,0:T(8,128)(2,1)S(1)} %get-tuple-element.73), channel_id=1, source_target_pairs={{0,128},{32,160},{64,192},{96,224},{128,0},{160,32},{192,64},{224,... | collective-permute-start | bytes 208904 | tf_op jit(solution)/shard_map/ppermute | solution.py:306
  46.0 0.0 collective-permute-done
  46.1 1.9 %collective-permute-start.4 = (bf16[2,34,8,128]{3,2,1,0:T(8,128)(2,1)S(1)}, bf16[2,34,8,128]{3,2,1,0:T(8,128)(2,1)S(1)}, u32[]{:S(2)}, u32[]{:S(2)}) collective-permute-start(bf16[2,34,8,128]{3,2,1,0:T(8,128)(2,1)S(1)} %pad_maximum_fusion.2), channel_id=1, source_target_pairs={{0,32},{16,240},{32,64},{48,16},{64,96},{80,48},{96,128},{112,80},... | collective-permute-start | bytes 417800 | tf_op jit(solution)/shard_map/ppermute | solution.py:314
  48.0 2.1 %collective-permute-start.5 = (bf16[2,34,8,128]{3,2,1,0:T(8,128)(2,1)S(1)}, bf16[2,34,8,128]{3,2,1,0:T(8,128)(2,1)S(1)}, u32[]{:S(2)}, u32[]{:S(2)}) collective-permute-start(bf16[2,34,8,128]{3,2,1,0:T(8,128)(2,1)S(1)} %pad_maximum_fusion.3), channel_id=1, source_target_pairs={{0,64},{16,208},{32,96},{48,240},{64,128},{80,16},{96,160},{112,48... | collective-permute-start | bytes 417800 | tf_op jit(solution)/shard_map/ppermute | solution.py:314
  50.1 1.3 %collective-permute-start.1 = (bf16[2,34,8,128]{3,2,1,0:T(8,128)(2,1)S(1)}, bf16[2,34,8,128]{3,2,1,0:T(8,128)(2,1)S(1)}, u32[]{:S(2)}, u32[]{:S(2)}) collective-permute-start(bf16[2,34,8,128]{3,2,1,0:T(8,128)(2,1)S(1)} %pad_maximum_fusion.1), channel_id=1, source_target_pairs={{0,96},{16,176},{32,128},{48,208},{64,160},{80,240},{96,192},{112,... | collective-permute-start | bytes 417800 | tf_op jit(solution)/shard_map/ppermute | solution.py:314
  51.3 0.7 collective-permute-done.4
  52.0 6.0 %collective-permute-done.5 = bf16[2,34,8,128]{3,2,1,0:T(8,128)(2,1)S(1)} collective-permute-done((bf16[2,34,8,128]{3,2,1,0:T(8,128)(2,1)S(1)}, bf16[2,34,8,128]{3,2,1,0:T(8,128)(2,1)S(1)}, u32[]{:S(2)}, u32[]{:S(2)}) %collective-permute-start.5) | collective-permute-done | bytes 139296 | tf_op jit(solution)/shard_map/ppermute | solution.py:314
  58.0 0.1 copy.27
  58.1 1.8 %collective-permute-start.6 = (bf16[34,40,128]{2,1,0:T(8,128)(2,1)S(1)}, bf16[34,40,128]{2,1,0:T(8,128)(2,1)S(1)}, u32[]{:S(2)}, u32[]{:S(2)}) collective-permute-start(bf16[34,40,128]{2,1,0:T(8,128)(2,1)S(1)} %bitcast.41), channel_id=1, source_target_pairs={{0,3},{1,2},{2,1},{3,0},{4,7},{5,6},{6,5},{7,4},{8,11},{9,10},{10,... | collective-permute-start | bytes 1044488 | tf_op jit(solution)/shard_map/ppermute | solution.py:325
  59.9 0.0 collective-permute-done.1
  59.9 0.0 collective-permute-done.2
  60.0 1.1 %collective-permute-start.3 = (bf16[34,24,128]{2,1,0:T(8,128)(2,1)S(1)}, bf16[34,24,128]{2,1,0:T(8,128)(2,1)S(1)}, u32[]{:S(2)}, u32[]{:S(2)}) collective-permute-start(bf16[34,24,128]{2,1,0:T(8,128)(2,1)S(1)} %copy_bitcast_fusion.1.refs_1_), channel_id=1, source_target_pairs={{0,3},{1,2},{2,1},{3,0},{4,7},{5,6},{6,5},{7,4},{8,11},{9,10},{10,... | collective-permute-start | bytes 626696 | tf_op jit(solution)/shard_map/ppermute | solution.py:325
  61.0 4.8 %collective-permute-start.7 = (bf16[34,40,128]{2,1,0:T(8,128)(2,1)S(1)}, bf16[34,40,128]{2,1,0:T(8,128)(2,1)S(1)}, u32[]{:S(2)}, u32[]{:S(2)}) collective-permute-start(bf16[34,40,128]{2,1,0:T(8,128)(2,1)S(1)} %bitcast.42), channel_id=1, source_target_pairs={{0,16},{16,0},{1,17},{17,1},{2,18},{18,2},{3,19},{19,3},{4,20},{20... | collective-permute-start | bytes 1044488 | tf_op jit(solution)/shard_map/ppermute | solution.py:326
  65.9 3.7 %collective-permute-done.6.refs_2_ = bf16[34,40,128]{2,1,0:T(8,128)(2,1)S(1)} collective-permute-done((bf16[34,40,128]{2,1,0:T(8,128)(2,1)S(1)}, bf16[34,40,128]{2,1,0:T(8,128)(2,1)S(1)}, u32[]{:S(2)}, u32[]{:S(2)}) %collective-permute-start.6) | collective-permute-done | bytes 348192 | tf_op jit(solution)/shard_map/ppermute | solution.py:325
  69.6 0.0 collective-permute-start.9
  69.6 0.5 collective-permute-start.8
  70.1 0.0 all-to-all-done.2.x_ref
  70.1 2.9 %collective-permute-done.3.refs_3_ = bf16[34,24,128]{2,1,0:T(8,128)(2,1)S(1)} collective-permute-done((bf16[34,24,128]{2,1,0:T(8,128)(2,1)S(1)}, bf16[34,24,128]{2,1,0:T(8,128)(2,1)S(1)}, u32[]{:S(2)}, u32[]{:S(2)}) %collective-permute-start.3) | collective-permute-done | bytes 208928 | tf_op jit(solution)/shard_map/ppermute | solution.py:325
  73.0 0.0 collective-permute-start.10
  73.0 0.0 collective-permute-done.8.refs_5_
  73.1 0.0 collective-permute-done.7.refs_4_
  73.1 1.4 %collective-permute-done.10.refs_7_ = bf16[34,24,128]{2,1,0:T(8,128)(2,1)S(1)} collective-permute-done((bf16[34,24,128]{2,1,0:T(8,128)(2,1)S(1)}, bf16[34,24,128]{2,1,0:T(8,128)(2,1)S(1)}, u32[]{:S(2)}, u32[]{:S(2)}) %collective-permute-start.10) | collective-permute-done | bytes 208928 | tf_op jit(solution)/shard_map/ppermute | solution.py:329
  74.5 0.0 collective-permute-done.9.refs_6_
  74.5 5.1 %shard_map.81 = (bf16[128,512]{1,0:T(8,128)(2,1)S(1)}, bf16[128,512]{1,0:T(8,128)(2,1)S(1)}, bf16[128,512]{1,0:T(8,128)(2,1)S(1)}, bf16[128,512]{1,0:T(8,128)(2,1)S(1)}) custom-call(s32[8,8]{1,0:T(8,128)S(1)} %get-tuple-element.69.slots_ref, bf16[8,128,768]{2,1,0:T(8,128)(2,1)S(1)} %all-to-all-done.2.x_ref, bf16[34,40,128]{2,1,0:T(8,128)(2,1)S(1)} %bitcast.43, ...), custom_call_target="tpu_custom_call" | custom-call | flops 1073741824 | bytes 2097152 | tf_op jit(solution)/shard_map/pallas_call | solution.py:333
  79.6 2.9 %collective-permute-start.14 = (bf16[128,512]{1,0:T(8,128)(2,1)S(1)}, bf16[128,512]{1,0:T(8,128)(2,1)}, u32[]{:S(2)}, u32[]{:S(2)}) collective-permute-start(bf16[128,512]{1,0:T(8,128)(2,1)S(1)} %get-tuple-element.80), channel_id=1, source_target_pairs={{0,8},{1,9},{4,12},{5,13},{8,0},{9,1},{12,4},{13,5},{2,10},{3,11},... | collective-permute-start | bytes 393224 | tf_op jit(solution)/shard_map/ppermute | solution.py:347
  82.5 0.0 collective-permute-start.15
  82.5 2.4 %collective-permute-start.16 = (bf16[128,512]{1,0:T(8,128)(2,1)S(1)}, bf16[128,512]{1,0:T(8,128)(2,1)}, u32[]{:S(2)}, u32[]{:S(2)}) collective-permute-start(bf16[128,512]{1,0:T(8,128)(2,1)S(1)} %get-tuple-element.82), channel_id=1, source_target_pairs={{0,12},{1,13},{4,8},{5,9},{8,4},{9,5},{12,0},{13,1},{2,14},{3,15},... | collective-permute-start | bytes 393224 | tf_op jit(solution)/shard_map/ppermute | solution.py:347
  84.9 1.5 %collective-permute-start.17 = (bf16[128,512]{1,0:T(8,128)(2,1)S(1)}, bf16[128,512]{1,0:T(8,128)(2,1)}, u32[]{:S(2)}, u32[]{:S(2)}) collective-permute-start(bf16[128,512]{1,0:T(8,128)(2,1)S(1)} %get-tuple-element.83), channel_id=1, source_target_pairs={{0,13},{1,12},{4,9},{5,8},{8,5},{9,4},{12,1},{13,0},{2,15},{3,14},... | collective-permute-start | bytes 393224 | tf_op jit(solution)/shard_map/ppermute | solution.py:347
  86.4 4.1 %shard_map.80 = (bf16[128,512]{1,0:T(8,128)(2,1)S(1)}, bf16[128,512]{1,0:T(8,128)(2,1)S(1)}, bf16[128,512]{1,0:T(8,128)(2,1)S(1)}) custom-call(s32[8,8]{1,0:T(8,128)S(1)} %get-tuple-element.69.slots_ref, bf16[8,128,768]{2,1,0:T(8,128)(2,1)S(1)} %all-to-all-done.2.x_ref, bf16[34,40,128]{2,1,0:T(8,128)(2,1)S(1)} %bitcast.44, ...), custom_call_target="tpu_custom_call" | custom-call | flops 1073741824 | bytes 2097152 | tf_op jit(solution)/shard_map/pallas_call | solution.py:333
  90.5 0.1 collective-permute-start.11
  90.6 0.0 collective-permute-done.14
  90.6 0.1 collective-permute-start.12
  90.7 0.0 collective-permute-done.15
  90.7 2.5 %collective-permute-start.13 = (bf16[128,512]{1,0:T(8,128)(2,1)S(1)}, bf16[128,512]{1,0:T(8,128)(2,1)}, u32[]{:S(2)}, u32[]{:S(2)}) collective-permute-start(bf16[128,512]{1,0:T(8,128)(2,1)S(1)} %get-tuple-element.79), channel_id=1, source_target_pairs={{0,5},{1,4},{4,1},{5,0},{8,13},{9,12},{12,9},{13,8},{2,7},{3,6},{6... | collective-permute-start | bytes 393224 | tf_op jit(solution)/shard_map/ppermute | solution.py:347
  93.8 0.0 copy-start.7
  93.9 0.0 copy-start.8
  93.9 2.7 %shard_map.79 = bf16[128,512]{1,0:T(8,128)(2,1)} custom-call(s32[8,8]{1,0:T(8,128)S(1)} %get-tuple-element.69.slots_ref, bf16[8,128,768]{2,1,0:T(8,128)(2,1)S(1)} %all-to-all-done.2.x_ref, bf16[34,40,128]{2,1,0:T(8,128)(2,1)S(1)} %bitcast.45, bf16[34,24,128]{2,1,0:T(8,128)(2,1)S(1)} %copy_bitcast_fusion.1.refs_1_, ...), custom_call_target="tpu_custom_call" | custom-call | flops 1073741824 | bytes 2097152 | tf_op jit(solution)/shard_map/pallas_call | solution.py:333
  96.6 0.0 collective-permute-done.16
  96.6 0.0 collective-permute-done.17
  96.6 0.0 collective-permute-done.11
  96.6 0.0 collective-permute-done.12
  96.6 0.3 collective-permute-done.13
  96.9 0.0 copy-done.7
  96.9 0.0 copy-done.8
  96.9 2.1 %conditional.1 = (bf16[128,4096]{1,0:T(8,128)(2,1)}) conditional(s32[]{:T(128)} %bitcast.9, (s32[32768]{0:T(1024)S(1)}, s32[256,8]{0,1:T(8,128)S(1)}, bf16[8,128,768]{2,1,0:T(8,128)(2,1)}, bf16[256,8,128]{2,1,0:T(8,128)(2,1)}) %tuple.33, (bf16[128,512]{1,0:T(8,128)(2,1)}, bf16[128,512]{1,0:T(8,128)(2,1)}, bf16[128,512]{1,0:T(8,128)(2,1)}, ...), branch_computations={%region_0.3_spmd, %region_3.4_spmd} | conditional | flops 2829850 | bytes 42080624 | solution.py:447
  96.9 2.1 %branch_1_fun.1 = bf16[128,4096]{1,0:T(8,128)(2,1)} custom-call(bf16[128,512]{1,0:T(8,128)(2,1)} %get-tuple-element.36.refs_0_, bf16[128,512]{1,0:T(8,128)(2,1)} %get-tuple-element.37.refs_1_, bf16[128,512]{1,0:T(8,128)(2,1)} %get-tuple-element.38.refs_2_, bf16[128,512]{1,0:T(8,128)(2,1)} %get-tuple-element.39.refs_3_, ...), custom_call_target="tpu_custom_call" | custom-call | tf_op jit(solution)/shard_map/cond/branch_1_fun/pallas_call | solution.py:352
  (14 shorter events, 0.2 us)
Async XLA Ops:
  0.0 20.7 %copy-start = (bf16[128,1024]{1,0:T(8,128)(2,1)S(1)}, bf16[128,1024]{1,0:T(8,128)(2,1)}, u32[]{:S(2)}) copy-start(bf16[128,1024]{1,0:T(8,128)(2,1)} %v_ref.1) | copy-start | bytes 786436
  0.0 20.7 %copy-start.1 = (bf16[128,4096]{1,0:T(8,128)(2,1)S(1)}, bf16[128,4096]{1,0:T(8,128)(2,1)}, u32[]{:S(2)}) copy-start(bf16[128,4096]{1,0:T(8,128)(2,1)} %q_ref.1) | copy-start | bytes 3145732
  2.9 36.5 %all-to-all-start.1 = ((bf16[256,8,128]{2,1,0:T(8,128)(2,1)}), bf16[256,8,128]{2,1,0:T(8,128)(2,1)S(1)}, u32[]{:S(2)}, u32[]{:S(2)}) async-start(bf16[256,8,128]{2,1,0:T(8,128)(2,1)} %bitcast.50), calls=%async_computation.1 | async-start | bytes 1048576 | tf_op jit(solution)/shard_map/all_to_all | solution.py:416
  20.7 1.0 copy-start.2
  21.6 0.8 copy-start.3
  22.5 0.8 copy-start.4
  39.4 4.9 %copy-start.5 = (bf16[256,8,128]{2,1,0:T(8,128)(2,1)}, bf16[256,8,128]{2,1,0:T(8,128)(2,1)S(1)}, u32[]{:S(2)}) copy-start(bf16[256,8,128]{2,1,0:T(8,128)(2,1)S(1)} %all-to-all-done.1.src_ref) | copy-start | bytes 1572868
  39.4 30.7 %all-to-all-start.2 = ((bf16[8,128,768]{2,1,0:T(8,128)(2,1)}), bf16[8,128,768]{2,1,0:T(8,128)(2,1)S(1)}, u32[]{:S(2)}, u32[]{:S(2)}) async-start(bf16[8,128,768]{2,1,0:T(8,128)(2,1)} %shard_map.77), calls=%async_computation.2 | async-start | bytes 3145728 | tf_op jit(solution)/shard_map/all_to_all | solution.py:444
  44.3 1.8 %collective-permute-start = (bf16[3,34,8,128]{3,2,1,0:T(8,128)(2,1)S(1)}, bf16[3,34,8,128]{3,2,1,0:T(8,128)(2,1)S(1)}, u32[]{:S(2)}, u32[]{:S(2)}) collective-permute-start(bf16[3,34,8,128]{3,2,1,0:T(8,128)(2,1)S(1)} %get-tuple-element.72), channel_id=1, source_target_pairs={{0,16},{16,0},{1,17},{17,1},{2,18},{18,2},{3,19},{19,3},{4,20},{20... | collective-permute-start | bytes 626696 | tf_op jit(solution)/shard_map/ppermute | solution.py:305
  44.5 15.5 %collective-permute-start.2 = (bf16[34,8,128]{2,1,0:T(8,128)(2,1)S(1)}, bf16[34,8,128]{2,1,0:T(8,128)(2,1)S(1)}, u32[]{:S(2)}, u32[]{:S(2)}) collective-permute-start(bf16[34,8,128]{2,1,0:T(8,128)(2,1)S(1)} %get-tuple-element.73), channel_id=1, source_target_pairs={{0,128},{32,160},{64,192},{96,224},{128,0},{160,32},{192,64},{224,... | collective-permute-start | bytes 208904 | tf_op jit(solution)/shard_map/ppermute | solution.py:306
  46.1 5.9 %collective-permute-start.4 = (bf16[2,34,8,128]{3,2,1,0:T(8,128)(2,1)S(1)}, bf16[2,34,8,128]{3,2,1,0:T(8,128)(2,1)S(1)}, u32[]{:S(2)}, u32[]{:S(2)}) collective-permute-start(bf16[2,34,8,128]{3,2,1,0:T(8,128)(2,1)S(1)} %pad_maximum_fusion.2), channel_id=1, source_target_pairs={{0,32},{16,240},{32,64},{48,16},{64,96},{80,48},{96,128},{112,80},... | collective-permute-start | bytes 417800 | tf_op jit(solution)/shard_map/ppermute | solution.py:314
  48.0 10.0 %collective-permute-start.5 = (bf16[2,34,8,128]{3,2,1,0:T(8,128)(2,1)S(1)}, bf16[2,34,8,128]{3,2,1,0:T(8,128)(2,1)S(1)}, u32[]{:S(2)}, u32[]{:S(2)}) collective-permute-start(bf16[2,34,8,128]{3,2,1,0:T(8,128)(2,1)S(1)} %pad_maximum_fusion.3), channel_id=1, source_target_pairs={{0,64},{16,208},{32,96},{48,240},{64,128},{80,16},{96,160},{112,48... | collective-permute-start | bytes 417800 | tf_op jit(solution)/shard_map/ppermute | solution.py:314
  50.1 9.8 %collective-permute-start.1 = (bf16[2,34,8,128]{3,2,1,0:T(8,128)(2,1)S(1)}, bf16[2,34,8,128]{3,2,1,0:T(8,128)(2,1)S(1)}, u32[]{:S(2)}, u32[]{:S(2)}) collective-permute-start(bf16[2,34,8,128]{3,2,1,0:T(8,128)(2,1)S(1)} %pad_maximum_fusion.1), channel_id=1, source_target_pairs={{0,96},{16,176},{32,128},{48,208},{64,160},{80,240},{96,192},{112,... | collective-permute-start | bytes 417800 | tf_op jit(solution)/shard_map/ppermute | solution.py:314
  58.1 11.5 %collective-permute-start.6 = (bf16[34,40,128]{2,1,0:T(8,128)(2,1)S(1)}, bf16[34,40,128]{2,1,0:T(8,128)(2,1)S(1)}, u32[]{:S(2)}, u32[]{:S(2)}) collective-permute-start(bf16[34,40,128]{2,1,0:T(8,128)(2,1)S(1)} %bitcast.41), channel_id=1, source_target_pairs={{0,3},{1,2},{2,1},{3,0},{4,7},{5,6},{6,5},{7,4},{8,11},{9,10},{10,... | collective-permute-start | bytes 1044488 | tf_op jit(solution)/shard_map/ppermute | solution.py:325
  60.0 13.1 %collective-permute-start.3 = (bf16[34,24,128]{2,1,0:T(8,128)(2,1)S(1)}, bf16[34,24,128]{2,1,0:T(8,128)(2,1)S(1)}, u32[]{:S(2)}, u32[]{:S(2)}) collective-permute-start(bf16[34,24,128]{2,1,0:T(8,128)(2,1)S(1)} %copy_bitcast_fusion.1.refs_1_), channel_id=1, source_target_pairs={{0,3},{1,2},{2,1},{3,0},{4,7},{5,6},{6,5},{7,4},{8,11},{9,10},{10,... | collective-permute-start | bytes 626696 | tf_op jit(solution)/shard_map/ppermute | solution.py:325
  61.0 12.0 %collective-permute-start.7 = (bf16[34,40,128]{2,1,0:T(8,128)(2,1)S(1)}, bf16[34,40,128]{2,1,0:T(8,128)(2,1)S(1)}, u32[]{:S(2)}, u32[]{:S(2)}) collective-permute-start(bf16[34,40,128]{2,1,0:T(8,128)(2,1)S(1)} %bitcast.42), channel_id=1, source_target_pairs={{0,16},{16,0},{1,17},{17,1},{2,18},{18,2},{3,19},{19,3},{4,20},{20... | collective-permute-start | bytes 1044488 | tf_op jit(solution)/shard_map/ppermute | solution.py:326
  69.6 4.9 %collective-permute-start.9 = (bf16[34,40,128]{2,1,0:T(8,128)(2,1)S(1)}, bf16[34,40,128]{2,1,0:T(8,128)(2,1)S(1)}, u32[]{:S(2)}, u32[]{:S(2)}) collective-permute-start(bf16[34,40,128]{2,1,0:T(8,128)(2,1)S(1)} %collective-permute-done.6.refs_2_), channel_id=1, source_target_pairs={{0,16},{16,0},{1,17},{17,1},{2,18},{18,2},{3,19},{19,3},{4,20},{20... | collective-permute-start | bytes 1044488 | tf_op jit(solution)/shard_map/ppermute | solution.py:329
  69.6 3.5 %collective-permute-start.8 = (bf16[34,24,128]{2,1,0:T(8,128)(2,1)S(1)}, bf16[34,24,128]{2,1,0:T(8,128)(2,1)}, u32[]{:S(2)}, u32[]{:S(2)}) collective-permute-start(bf16[34,24,128]{2,1,0:T(8,128)(2,1)S(1)} %copy_bitcast_fusion.1.refs_1_), channel_id=1, source_target_pairs={{0,16},{16,0},{1,17},{17,1},{2,18},{18,2},{3,19},{19,3},{4,20},{20... | collective-permute-start | bytes 626696 | tf_op jit(solution)/shard_map/ppermute | solution.py:326
  73.0 1.5 %collective-permute-start.10 = (bf16[34,24,128]{2,1,0:T(8,128)(2,1)S(1)}, bf16[34,24,128]{2,1,0:T(8,128)(2,1)S(1)}, u32[]{:S(2)}, u32[]{:S(2)}) collective-permute-start(bf16[34,24,128]{2,1,0:T(8,128)(2,1)S(1)} %collective-permute-done.3.refs_3_), channel_id=1, source_target_pairs={{0,16},{16,0},{1,17},{17,1},{2,18},{18,2},{3,19},{19,3},{4,20},{20... | collective-permute-start | bytes 626696 | tf_op jit(solution)/shard_map/ppermute | solution.py:329
  79.6 11.0 %collective-permute-start.14 = (bf16[128,512]{1,0:T(8,128)(2,1)S(1)}, bf16[128,512]{1,0:T(8,128)(2,1)}, u32[]{:S(2)}, u32[]{:S(2)}) collective-permute-start(bf16[128,512]{1,0:T(8,128)(2,1)S(1)} %get-tuple-element.80), channel_id=1, source_target_pairs={{0,8},{1,9},{4,12},{5,13},{8,0},{9,1},{12,4},{13,5},{2,10},{3,11},... | collective-permute-start | bytes 393224 | tf_op jit(solution)/shard_map/ppermute | solution.py:347
  82.5 8.2 %collective-permute-start.15 = (bf16[128,512]{1,0:T(8,128)(2,1)S(1)}, bf16[128,512]{1,0:T(8,128)(2,1)}, u32[]{:S(2)}, u32[]{:S(2)}) collective-permute-start(bf16[128,512]{1,0:T(8,128)(2,1)S(1)} %get-tuple-element.81), channel_id=1, source_target_pairs={{0,9},{1,8},{4,13},{5,12},{8,1},{9,0},{12,5},{13,4},{2,11},{3,10},... | collective-permute-start | bytes 393224 | tf_op jit(solution)/shard_map/ppermute | solution.py:347
  82.5 14.0 %collective-permute-start.16 = (bf16[128,512]{1,0:T(8,128)(2,1)S(1)}, bf16[128,512]{1,0:T(8,128)(2,1)}, u32[]{:S(2)}, u32[]{:S(2)}) collective-permute-start(bf16[128,512]{1,0:T(8,128)(2,1)S(1)} %get-tuple-element.82), channel_id=1, source_target_pairs={{0,12},{1,13},{4,8},{5,9},{8,4},{9,5},{12,0},{13,1},{2,14},{3,15},... | collective-permute-start | bytes 393224 | tf_op jit(solution)/shard_map/ppermute | solution.py:347
  84.9 11.6 %collective-permute-start.17 = (bf16[128,512]{1,0:T(8,128)(2,1)S(1)}, bf16[128,512]{1,0:T(8,128)(2,1)}, u32[]{:S(2)}, u32[]{:S(2)}) collective-permute-start(bf16[128,512]{1,0:T(8,128)(2,1)S(1)} %get-tuple-element.83), channel_id=1, source_target_pairs={{0,13},{1,12},{4,9},{5,8},{8,5},{9,4},{12,1},{13,0},{2,15},{3,14},... | collective-permute-start | bytes 393224 | tf_op jit(solution)/shard_map/ppermute | solution.py:347
  90.5 6.1 %collective-permute-start.11 = (bf16[128,512]{1,0:T(8,128)(2,1)S(1)}, bf16[128,512]{1,0:T(8,128)(2,1)}, u32[]{:S(2)}, u32[]{:S(2)}) collective-permute-start(bf16[128,512]{1,0:T(8,128)(2,1)S(1)} %get-tuple-element.77), channel_id=1, source_target_pairs={{0,1},{1,0},{4,5},{5,4},{8,9},{9,8},{12,13},{13,12},{2,3},{3,2},{6... | collective-permute-start | bytes 393224 | tf_op jit(solution)/shard_map/ppermute | solution.py:347
  90.6 6.0 %collective-permute-start.12 = (bf16[128,512]{1,0:T(8,128)(2,1)S(1)}, bf16[128,512]{1,0:T(8,128)(2,1)}, u32[]{:S(2)}, u32[]{:S(2)}) collective-permute-start(bf16[128,512]{1,0:T(8,128)(2,1)S(1)} %get-tuple-element.78), channel_id=1, source_target_pairs={{0,4},{1,5},{4,0},{5,1},{8,12},{9,13},{12,8},{13,9},{2,6},{3,7},{6... | collective-permute-start | bytes 393224 | tf_op jit(solution)/shard_map/ppermute | solution.py:347
  90.7 6.2 %collective-permute-start.13 = (bf16[128,512]{1,0:T(8,128)(2,1)S(1)}, bf16[128,512]{1,0:T(8,128)(2,1)}, u32[]{:S(2)}, u32[]{:S(2)}) collective-permute-start(bf16[128,512]{1,0:T(8,128)(2,1)S(1)} %get-tuple-element.79), channel_id=1, source_target_pairs={{0,5},{1,4},{4,1},{5,0},{8,13},{9,12},{12,9},{13,8},{2,7},{3,6},{6... | collective-permute-start | bytes 393224 | tf_op jit(solution)/shard_map/ppermute | solution.py:347
  93.8 3.1 %copy-start.7 = (s32[32768]{0:T(1024)S(1)}, s32[32768]{0:T(1024)}, u32[]{:S(2)}) copy-start(s32[32768]{0:T(1024)} %param.13) | copy-start | bytes 393220
  93.9 3.0 %copy-start.8 = (s32[256,8]{0,1:T(8,128)S(1)}, s32[256,8]{0,1:T(8,128)}, u32[]{:S(2)}) copy-start(s32[256,8]{0,1:T(8,128)} %param.12) | copy-start | bytes 24580
